TPU v7x, 256 devices: a whole 4x4x8 slice. The times are simulated.
256 devices in a mesh: seq: 64 (over z, y, core), ch: 4 (over x).
Axes of the slice: x: 4, y: 4, z: 8, core: 2. Of those that a mesh axis runs over, the one named last changes fastest.
Arguments:
- streams: bfloat16 [3, 8192, 4096], P(None, 'seq', 'ch'), may hold values from -6 to 6
- short_taps: float32 [3, 3, 4096], P(None, None, 'ch'), may hold values from -2.5 to 2.5
- long_filter: float32 [8192, 4096], P('seq', 'ch'), may hold values from -10 to 10
- skip_bias: float32 [4096], P('ch'), may hold values from -2.5 to 2.5
- norm_gain: float32 [4096], P('ch'), may hold values from 0.5 to 1.5
- cotangent: bfloat16 [8192, 4096], P('seq', 'ch'), may hold values from -6 to 6
Outputs:
- normed: bfloat16 [8192, 4096], P('seq', 'ch')
- stream_grads: bfloat16 [3, 8192, 4096], P(None, 'seq', 'ch')
All inputs are finite; a program needn't handle non-finite values.
Results may differ from a plain program's by a relative error of at most 0.001.
Values sent between devices are 32-bit elements; how exact they have to be, the bound alone decides.
A program may use at most 64 MiB of HBM per device.

v0:
```python
import math

import jax
import jax.numpy as jnp
from jax import lax
from jax.sharding import PartitionSpec as P

EXACTNESS = lax.Precision.HIGHEST


def passed_along(block, axis, distance):
    devices = range(lax.axis_size(axis))
    route = [(i - distance, i) for i in devices if i - distance in devices]
    return lax.ppermute(block, axis, route)


def counting(amount):
    return jnp.arange(amount, dtype=jnp.int32)


def angle_pair(left_index, right_index, period, turning):
    product = left_index[:, None] * right_index[None, :] % period
    angles = product.astype(jnp.float32) * (turning * 2.0 * math.pi / period)
    return (jnp.cos(angles), jnp.sin(angles))


def neighbour_rows(edge_rows, offset):
    return passed_along(edge_rows, "seq", offset)


def swap_blocks(blocks):
    return lax.all_to_all(blocks, "seq", split_axis=1, concat_axis=0, tiled=True)


def spread_forward(series):
    length, series_count, chan_width = series.shape
    devices = lax.axis_size("seq")
    position = lax.axis_index("seq")
    sub_rows = length // devices
    period = 2 * length * devices
    gathered = swap_blocks(series.reshape(1, length, series_count, chan_width))
    cos_a, sin_a = angle_pair(counting(2 * devices), counting(devices), 2 * devices, -1.0)
    real_part = jnp.einsum("ka,absc->bksc", cos_a, gathered, precision=EXACTNESS)
    imag_part = jnp.einsum("ka,absc->bksc", sin_a, gathered, precision=EXACTNESS)
    spike_locations = position * sub_rows + counting(sub_rows)
    turn_cos, turn_sin = angle_pair(spike_locations, counting(2 * devices), period, -1.0)
    turn_cos = turn_cos[:, :, None, None]
    turn_sin = turn_sin[:, :, None, None]
    turned = jnp.concatenate(
        [real_part * turn_cos - imag_part * turn_sin, real_part * turn_sin + imag_part * turn_cos],
        axis=2,
    )
    swapped = swap_blocks(turned)
    cos_b, sin_b = angle_pair(counting(length), counting(length), length, -1.0)
    primary = jnp.einsum("jb,bksc->jksc", cos_b, swapped, precision=EXACTNESS)
    second = jnp.einsum("jb,bksc->jksc", sin_b, swapped, precision=EXACTNESS)
    return (
        primary[:, :, :series_count] - second[:, :, series_count:],
        primary[:, :, series_count:] + second[:, :, :series_count],
    )


def spread_inverse(spec_re, spec_im):
    length, pair_rows, series_count, chan_width = spec_re.shape
    devices = lax.axis_size("seq")
    position = lax.axis_index("seq")
    sub_rows = length // devices
    period = 2 * length * devices
    cos_b, sin_b = angle_pair(counting(length), counting(length), length, 1.0)
    merged = jnp.concatenate([spec_re, spec_im], axis=2)
    primary = jnp.einsum("bj,jksc->kbsc", cos_b, merged, precision=EXACTNESS)
    second = jnp.einsum("bj,jksc->kbsc", sin_b, merged, precision=EXACTNESS)
    turned = jnp.concatenate(
        [
            primary[:, :, :series_count] - second[:, :, series_count:],
            primary[:, :, series_count:] + second[:, :, :series_count],
        ],
        axis=2,
    )
    swapped = swap_blocks(turned)
    spike_locations = position * sub_rows + counting(sub_rows)
    turn_cos, turn_sin = angle_pair(counting(2 * devices), spike_locations, period, 1.0)
    turn_cos = turn_cos[:, :, None, None]
    turn_sin = turn_sin[:, :, None, None]
    real_part = swapped[:, :, :series_count]
    imag_part = swapped[:, :, series_count:]
    rotated_re = real_part * turn_cos - imag_part * turn_sin
    rotated_im = real_part * turn_sin + imag_part * turn_cos
    cos_a, sin_a = angle_pair(counting(devices), counting(2 * devices), 2 * devices, 1.0)
    result = jnp.einsum("ak,kbsc->basc", cos_a, rotated_re, precision=EXACTNESS) - jnp.einsum(
        "ak,kbsc->basc", sin_a, rotated_im, precision=EXACTNESS
    )
    returned = swap_blocks(result / period)
    return returned.reshape(length, -1, chan_width)


def local(streams, short_taps, long_filter, skip_bias, norm_gain, cotangent):
    row_count = streams.shape[1]
    chan_width = streams.shape[2]
    rim_rows = short_taps.shape[1] - 1
    widened = streams.astype(jnp.float32)
    before = neighbour_rows(widened[:, row_count - rim_rows :, :], 1)
    extended = jnp.concatenate([before, widened], axis=1)
    shorts = jnp.zeros_like(widened)
    for offset in range(short_taps.shape[1]):
        shorts = (
            shorts
            + short_taps[:, offset, None, :]
            * extended[:, rim_rows - offset : rim_rows - offset + row_count, :]
        )
    short_q, short_k, short_v = (shorts[0], shorts[1], shorts[2])
    gated_input = short_k * short_v
    cot_wide = cotangent.astype(jnp.float32)
    carried = cot_wide * short_q
    series = jnp.stack([gated_input, long_filter, carried], axis=1)
    spec_re, spec_im = spread_forward(series)
    series_axis = 2
    gated_re = lax.index_in_dim(spec_re, 0, series_axis, keepdims=False)
    gated_im = lax.index_in_dim(spec_im, 0, series_axis, keepdims=False)
    filter_re = lax.index_in_dim(spec_re, 1, series_axis, keepdims=False)
    filter_im = lax.index_in_dim(spec_im, 1, series_axis, keepdims=False)
    carry_re = lax.index_in_dim(spec_re, 2, series_axis, keepdims=False)
    carry_im = lax.index_in_dim(spec_im, 2, series_axis, keepdims=False)
    output_re = filter_re * gated_re - filter_im * gated_im
    output_im = filter_re * gated_im + filter_im * gated_re
    backward_re = filter_re * carry_re + filter_im * carry_im
    backward_im = filter_re * carry_im - filter_im * carry_re
    inverse_re = jnp.stack([output_re, backward_re], axis=series_axis)
    inverse_im = jnp.stack([output_im, backward_im], axis=series_axis)
    result = spread_inverse(inverse_re, inverse_im)
    convolved = result[:, 0]
    correlated = result[:, 1]
    direct = convolved + skip_bias * gated_input
    mixed_out = short_q * direct
    square_sum = lax.psum(jnp.sum(mixed_out * mixed_out, axis=1), "ch")
    scaling = lax.rsqrt(square_sum[:, None] / (chan_width * lax.axis_size("ch")) + 1e-06)
    normed = (mixed_out * scaling * norm_gain).astype(jnp.bfloat16)
    gated_grad = correlated + skip_bias * carried
    short_grad = jnp.stack([cot_wide * direct, gated_grad * short_v, gated_grad * short_k])
    following = neighbour_rows(short_grad[:, :rim_rows, :], -1)
    grad_ext = jnp.concatenate([short_grad, following], axis=1)
    grads = jnp.zeros_like(short_grad)
    for offset in range(short_taps.shape[1]):
        grads = grads + short_taps[:, offset, None, :] * grad_ext[:, offset : offset + row_count, :]
    return (normed, grads.astype(jnp.bfloat16))


def solution(mesh):
    placed = (
        P(None, "seq", "ch"),
        P(None, None, "ch"),
        P("seq", "ch"),
        P("ch"),
        P("ch"),
        P("seq", "ch"),
    )
    return jax.shard_map(
        local,
        mesh=mesh,
        in_specs=placed,
        out_specs=(P("seq", "ch"), P(None, "seq", "ch")),
        check_vma=False,
    )
```

profile of v0, /device:TPU:1, one launch (start us, length us, event | category | flops | bytes accessed | tf_op | source)
XLA Modules:
  0.0 457.3 jit_solution(13354215304560620696)
XLA Ops:
  1.4 4.6 %collective-permute-start = (f32[3,2,1024]{2,1,0:T(2,128)S(1)}, f32[3,2,1024]{2,1,0:T(2,128)S(1)}, u32[]{:S(2)}, u32[]{:S(2)}) collective-permute-start(f32[3,2,1024]{2,1,0:T(2,128)S(1)} %slice.123), channel_id=1, source_target_pairs={{0,4},{4,8},{8,12},{12,16},{16,20},{20,24},{24,28},{28,32},{32,36}... | collective-permute-start | bytes 73736 | tf_op jit(solution)/shard_map/ppermute | solution.py:14
  6.0 0.9 fusion.133
  7.0 1.3 convert_element_type.52
  8.9 1.1 copy-done.1
  10.4 2.8 copy.64
  13.2 12.2 %all-to-all-start = ((f32[1,128,3,1024]{3,0,2,1:T(1,128)}), f32[1,128,3,1024]{3,0,2,1:T(1,128)S(1)}, u32[]{:S(2)}, u32[]{:S(2)}) async-start(f32[1,128,3,1024]{3,0,2,1:T(1,128)} %copy.64), calls=%async_computation | async-start | bytes 3145728 | tf_op jit(solution)/shard_map/all_to_all | solution.py:32
  25.6 38.7 %all-to-all-done = f32[1,128,3,1024]{3,0,2,1:T(1,128)S(1)} async-done(((f32[1,128,3,1024]{3,0,2,1:T(1,128)}), f32[1,128,3,1024]{3,0,2,1:T(1,128)S(1)}, u32[]{:S(2)}, u32[]{:S(2)}) %all-to-all-start) | async-done | bytes 1572896 | tf_op jit(solution)/shard_map/all_to_all | solution.py:32
  64.9 5.7 %fusion.25 = f32[2,3,1024,128]{3,2,1,0:T(8,128)S(1)} fusion(f32[64,2,3,1024]{3,2,1,0:T(4,128)S(1)} %bitcast.136), kind=kOutput, calls=%fused_computation.38 | convolution fusion | flops 604094464 | bytes 4718592 | tf_op jit(solution)/shard_map/ka,absc->bksc/dot_general | solution.py:44
  70.6 6.0 %subtract_bitcast_fusion = (f32[2,128,3,1024]{1,3,2,0:T(8,128)S(1)}, f32[2,128,3,1024]{1,3,2,0:T(8,128)S(1)}) fusion(f32[2,3,1024,128]{3,2,1,0:T(8,128)S(1)} %fusion.25, f32[2,128]{1,0:T(2,128)S(1)} %get-tuple-element.28, f32[2,128]{1,0:T(2,128)S(1)} %get-tuple-element.27, f32[64,2,3,1024]{3,2,1,0:T(4,128)S(1)} %bitcast.137), kind=kOutput, calls=%fused_computation.6 | convolution fusion | flops 608813056 | bytes 11012096 | tf_op jit(solution)/shard_map/ka,absc->bksc/dot_general | solution.py:43
  76.6 3.1 pad_maximum_fusion
  79.7 10.3 %copy.68 = f32[2,128,6,1024]{3,0,2,1:T(2,128)} copy(f32[2,128,6,1024]{1,3,2,0:T(8,128)} %pad_maximum_fusion) | data formatting | bytes 12582912 | tf_op jit(solution)/shard_map/concatenate | solution.py:49
  90.0 146.0 %all_to_all.63 = f32[2,128,6,1024]{3,0,2,1:T(2,128)S(1)} all-to-all(f32[2,128,6,1024]{3,0,2,1:T(2,128)} %copy.68), channel_id=1, replica_groups=mesh['seq'=64,'ch'=4] {'seq'}, dimensions={1} | all-to-all | bytes 12582912 | tf_op jit(solution)/shard_map/all_to_all | solution.py:32
  236.1 5.6 %copy.69 = f32[64,2,2,6,1024]{4,1,0,3,2:T(2,128)} copy(f32[64,2,2,6,1024]{4,1,3,2,0:T(2,128)S(1)} %bitcast.134) | data formatting | bytes 12582912 | tf_op jit(solution)/shard_map/all_to_all | solution.py:32
  241.7 8.5 %all_to_all.51 = f32[128,2,6,1024]{3,0,2,1:T(8,128)} reshape(f32[64,2,2,6,1024]{4,1,0,3,2:T(2,128)} %copy.69) | data formatting | bytes 12582912 | tf_op jit(solution)/shard_map/all_to_all | solution.py:32
  250.2 9.4 %fusion.40 = f32[128,2,6,1024]{3,0,2,1:T(8,128)S(1)} fusion(f32[128,2,6,1024]{3,0,2,1:T(8,128)} %all_to_all.51), kind=kOutput, calls=%fused_computation.71 | convolution fusion | flops 2416148480 | bytes 12582912 | tf_op jit(solution)/shard_map/jb,bksc->jksc/dot_general | solution.py:56
  259.6 6.4 %fusion.42 = f32[128,2,6,1024]{3,0,2,1:T(8,128)S(1)} fusion(f32[128,2,6,1024]{3,0,2,1:T(8,128)S(1)} %copy-done), kind=kOutput, calls=%fused_computation.73 | convolution fusion | flops 2416148480 | bytes 12582912 | tf_op jit(solution)/shard_map/jb,bksc->jksc/dot_general | solution.py:55
  266.0 2.2 slice_subtract_fusion
  268.9 7.2 %fusion.2 = f32[2,128,4,1024]{1,3,2,0:T(8,128)S(1)} fusion(f32[128,2,1,1024]{3,0,2,1:T(8,128)S(1)} %get-tuple-element.11, f32[128,2,1,1024]{3,0,2,1:T(8,128)S(1)} %get-tuple-element.13, f32[128,2,1,1024]{3,0,2,1:T(8,128)S(1)} %get-tuple-element.12, f32[128,2,1,1024]{3,0,2,1:T(8,128)S(1)} %get-tuple-element.10), kind=kOutput, calls=%fused_computation.9 | convolution fusion | flops 1613987840 | bytes 8388608 | tf_op jit(solution)/shard_map/bj,jksc->kbsc/dot_general | solution.py:71
  276.1 7.0 %fusion.3 = f32[2,128,4,1024]{1,3,2,0:T(8,128)S(1)} fusion(f32[128,2,1,1024]{3,0,2,1:T(8,128)S(1)} %get-tuple-element.11, f32[128,2,1,1024]{3,0,2,1:T(8,128)S(1)} %get-tuple-element.13, f32[128,2,1,1024]{3,0,2,1:T(8,128)S(1)} %get-tuple-element.12, f32[128,2,1,1024]{3,0,2,1:T(8,128)S(1)} %get-tuple-element.10), kind=kOutput, calls=%fused_computation.10 | convolution fusion | flops 1613987840 | bytes 8388608 | tf_op jit(solution)/shard_map/bj,jksc->kbsc/dot_general | solution.py:72
  283.5 2.3 pad_maximum_fusion.2
  285.8 5.5 %copy.72 = f32[2,128,4,1024]{3,2,0,1:T(4,128)} copy(f32[2,128,4,1024]{1,3,2,0:T(8,128)} %pad_maximum_fusion.2) | data formatting | bytes 8388608 | tf_op jit(solution)/shard_map/concatenate | solution.py:73
  291.3 7.4 %all-to-all-start.2 = ((f32[2,128,4,1024]{3,2,0,1:T(4,128)}), f32[2,128,4,1024]{3,2,0,1:T(4,128)}, u32[]{:S(2)}, u32[]{:S(2)}) async-start(f32[2,128,4,1024]{3,2,0,1:T(4,128)} %copy.72), calls=%async_computation.2 | async-start | bytes 8388608 | tf_op jit(solution)/shard_map/all_to_all | solution.py:32
  299.0 94.3 %all-to-all-done.2 = f32[2,128,4,1024]{3,2,0,1:T(4,128)} async-done(((f32[2,128,4,1024]{3,2,0,1:T(4,128)}), f32[2,128,4,1024]{3,2,0,1:T(4,128)}, u32[]{:S(2)}, u32[]{:S(2)}) %all-to-all-start.2) | async-done | bytes 4194336 | tf_op jit(solution)/shard_map/all_to_all | solution.py:32
  393.3 3.1 copy.74
  396.5 2.6 multiply_subtract_fusion
  399.1 2.5 fusion.4
  401.7 2.6 fusion.22
  405.1 34.9 %all_to_all.64 = f32[2,64,2,1024]{3,2,0,1:T(2,128)S(1)} all-to-all(f32[2,64,2,1024]{3,2,0,1:T(2,128)S(1)} %copy.79), channel_id=1, replica_groups=mesh['seq'=64,'ch'=4] {'seq'}, dimensions={1} | all-to-all | bytes 2097152 | tf_op jit(solution)/shard_map/all_to_all | solution.py:32
  441.6 3.3 collective-permute-start.1
  445.0 8.6 %psum.7 = f32[128]{0:T(128)S(1)} all-reduce(f32[128]{0:T(128)S(1)} %multiply_reduce_fusion), channel_id=1, replica_groups=mesh['seq'=64,'ch'=4] {'ch'}, use_global_device_ids=true, to_apply=%region_1.2 | all-reduce | flops 128 | bytes 1024 | tf_op jit(solution)/shard_map/psum | solution.py:135
  453.6 1.9 multiply_convert_fusion
  455.7 1.4 fusion.13
  (40 shorter events, 6.6 us)
Async XLA Ops:
  1.4 6.9 %collective-permute-start = (f32[3,2,1024]{2,1,0:T(2,128)S(1)}, f32[3,2,1024]{2,1,0:T(2,128)S(1)}, u32[]{:S(2)}, u32[]{:S(2)}) collective-permute-start(f32[3,2,1024]{2,1,0:T(2,128)S(1)} %slice.123), channel_id=1, source_target_pairs={{0,4},{4,8},{8,12},{12,16},{16,20},{20,24},{24,28},{28,32},{32,36}... | collective-permute-start | bytes 73736 | tf_op jit(solution)/shard_map/ppermute | solution.py:14
  8.3 1.7 copy-start.4
  8.8 1.2 copy-start.1
  8.9 1.4 copy-start.5
  13.2 51.1 %all-to-all-start = ((f32[1,128,3,1024]{3,0,2,1:T(1,128)}), f32[1,128,3,1024]{3,0,2,1:T(1,128)S(1)}, u32[]{:S(2)}, u32[]{:S(2)}) async-start(f32[1,128,3,1024]{3,0,2,1:T(1,128)} %copy.64), calls=%async_computation | async-start | bytes 3145728 | tf_op jit(solution)/shard_map/all_to_all | solution.py:32
  250.2 9.4 %copy-start = (f32[128,2,6,1024]{3,0,2,1:T(8,128)S(1)}, f32[128,2,6,1024]{3,0,2,1:T(8,128)}, u32[]{:S(2)}) copy-start(f32[128,2,6,1024]{3,0,2,1:T(8,128)} %all_to_all.51) | copy-start | bytes 18874372
  291.3 102.0 %all-to-all-start.2 = ((f32[2,128,4,1024]{3,2,0,1:T(4,128)}), f32[2,128,4,1024]{3,2,0,1:T(4,128)}, u32[]{:S(2)}, u32[]{:S(2)}) async-start(f32[2,128,4,1024]{3,2,0,1:T(4,128)} %copy.72), calls=%async_computation.2 | async-start | bytes 8388608 | tf_op jit(solution)/shard_map/all_to_all | solution.py:32
  405.1 35.8 %copy-start.2 = (f32[3,128,1024]{2,1,0:T(8,128)S(1)}, f32[3,128,1024]{2,1,0:T(8,128)}, u32[]{:S(2)}) copy-start(f32[3,128,1024]{2,1,0:T(8,128)} %copy-done.1) | copy-start | bytes 4718596
  405.1 35.8 %copy-start.7 = (f32[1024]{0:T(1024)S(1)}, f32[1024]{0:T(1024)}, u32[]{:S(2)}) copy-start(f32[1024]{0:T(1024)} %param.9) | copy-start | bytes 12292
  441.4 3.5 copy-start.3
  441.4 12.2 %copy-start.6 = (f32[1024]{0:T(1024)S(1)}, f32[1024]{0:T(1024)}, u32[]{:S(2)}) copy-start(f32[1024]{0:T(1024)} %param.10) | copy-start | bytes 12292
  441.6 13.9 %collective-permute-start.1 = (f32[3,2,1024]{2,1,0:T(2,128)S(1)}, f32[3,2,1024]{2,1,0:T(2,128)S(1)}, u32[]{:S(2)}, u32[]{:S(2)}) collective-permute-start(f32[3,2,1024]{2,1,0:T(2,128)S(1)} %slice.147), channel_id=1, source_target_pairs={{4,0},{8,4},{12,8},{16,12},{20,16},{24,20},{28,24},{32,28},{36,32}... | collective-permute-start | bytes 73736 | tf_op jit(solution)/shard_map/ppermute | solution.py:14
where the time goes:
time: 462 us; the launch traced here: 457 us
  blocking collectives  190 us (41%)
  waiting for transfers between devices  133 us (29%)
  matrix products  46.8 us (10%)
  local copies, waits for them, and re-layouts  41.5 us (9%)
  starting transfers between devices  27.5 us (6%)
  other arithmetic  17.8 us (4%)
    all_to_all x2, blocking collectives, swap_blocks(): lax.all_to_all(blocks, 'seq', split_axis=1, concat_axis=0, tiled=True)  181 us
    all_to_all x2, waiting for transfers between devices, swap_blocks(): lax.all_to_all(blocks, 'seq', split_axis=1, concat_axis=0, tiled=True)  133 us
    all_to_all x2, starting transfers between devices, swap_blocks(): lax.all_to_all(blocks, 'seq', split_axis=1, concat_axis=0, tiled=True)  19.6 us
    all_to_all x3, local copies, waits for them, and re-layouts, swap_blocks(): lax.all_to_all(blocks, 'seq', split_axis=1, concat_axis=0, tiled=True)  17.3 us
    concatenate x1, local copies, waits for them, and re-layouts, spread_forward(): jnp.concatenate([real_part * turn_cos - imag_part * turn_sin, real_part *...  10.3 us
    dot_general x1, matrix products, spread_forward(): second = jnp.einsum('jb,bksc->jksc', sin_b, swapped, precision=EXACTNESS)  9.37 us
  transfers between devices with their start and end apart: 4, of which 2 were waited for; matrix products, arithmetic and copies ran while one was open for 1% of the time, Pallas kernels for 0%

commit v1 on v0

v1 whole, which is shorter than its diff:
```python
import functools

import jax
import jax.numpy as jnp
import ml_dtypes
import numpy as np
from jax import lax
from jax.experimental import pallas as pl
from jax.experimental.pallas import tpu as pltpu
from jax.sharding import PartitionSpec as P

LANES = 128
ROWS = 8
WHOLE = pl.BlockSpec(memory_space=pltpu.VMEM)


def halves_of(table):
    high = table.astype(ml_dtypes.bfloat16)
    low = (table - high.astype(np.float64)).astype(ml_dtypes.bfloat16)
    return high, low


@functools.lru_cache(None)
def tables(devices, rows):
    length = devices * rows
    outer = np.arange(devices)
    inner = np.arange(rows)
    shifted = outer + 0.25
    angle = 2.0 * np.pi * np.outer(shifted, outer) / devices
    first = np.concatenate([np.cos(angle), -np.sin(angle)], axis=0)
    high, low = halves_of(first)
    first = np.concatenate([high, high, low], axis=1)
    last = np.concatenate([np.cos(angle).T, -np.sin(angle).T], axis=1) / length
    high, low = halves_of(last)
    last = np.concatenate([high, high, low], axis=1)
    turn = 2.0 * np.pi * np.outer(shifted, inner) / length
    turn = np.stack([np.cos(turn), -np.sin(turn)]).astype(np.float32)
    angle = 2.0 * np.pi * (np.outer(inner, inner) % rows) / rows
    cos, sin = np.cos(angle), np.sin(angle)
    high, low = halves_of(np.block([[cos, -sin], [sin, cos]]))
    forward = np.concatenate([high, high, low], axis=0)
    high, low = halves_of(np.block([[cos, sin], [-sin, cos]]))
    backward = np.concatenate([high, high, low], axis=0)
    return first, turn, forward, backward, last


def split(x):
    high = x.astype(jnp.bfloat16)
    low = (x - high.astype(jnp.float32)).astype(jnp.bfloat16)
    return high, low


def stacked_rows(x):
    high, low = split(x)
    return jnp.concatenate([high, low, high], axis=0)


def stacked_lanes(x):
    high, low = split(x)
    return jnp.concatenate([high, low, high], axis=1)


def product(a, b):
    return jnp.dot(a, b, preferred_element_type=jnp.float32)


def both_products(filtered, gated, carried, first, turn, forward, backward, last):
    devices = filtered.shape[0]
    turn_re, turn_im = turn[0], turn[1]
    joined = jnp.concatenate([filtered, gated, carried], axis=1)
    opened = product(first[...], stacked_rows(joined))
    parts = []
    for i in range(3):
        re = opened[:devices, i * LANES : (i + 1) * LANES]
        im = opened[devices:, i * LANES : (i + 1) * LANES]
        parts.append(
            jnp.concatenate([re * turn_re - im * turn_im, re * turn_im + im * turn_re], axis=1)
        )
    spectra = product(stacked_lanes(jnp.concatenate(parts, axis=0)), forward[...])
    filter_re, filter_im = spectra[:devices, :LANES], spectra[:devices, LANES:]
    gated_re, gated_im = spectra[devices : 2 * devices, :LANES], spectra[devices : 2 * devices, LANES:]
    carry_re, carry_im = spectra[2 * devices :, :LANES], spectra[2 * devices :, LANES:]
    forth = jnp.concatenate(
        [filter_re * gated_re - filter_im * gated_im, filter_re * gated_im + filter_im * gated_re],
        axis=1,
    )
    back = jnp.concatenate(
        [filter_re * carry_re + filter_im * carry_im, filter_re * carry_im - filter_im * carry_re],
        axis=1,
    )
    closed = product(stacked_lanes(jnp.concatenate([forth, back], axis=0)), backward[...])
    turned = []
    for i in range(2):
        re = closed[i * devices : (i + 1) * devices, :LANES]
        im = closed[i * devices : (i + 1) * devices, LANES:]
        turned.append(
            jnp.concatenate([re * turn_re + im * turn_im, im * turn_re - re * turn_im], axis=0)
        )
    result = product(last[...], stacked_rows(jnp.concatenate(turned, axis=1)))
    return result[:, :LANES], result[:, LANES:]


def spectral_kernel(devices, got, first, turn, forward, backward, last, out):
    for half in range(2):
        for c in range(ROWS):
            taken = [
                got[pl.ds((half * 3 + s) * ROWS + c, devices, stride=6 * ROWS), :] for s in range(3)
            ]
            results = both_products(*taken, first, turn, forward, backward, last)
            for s in range(2):
                out[pl.ds((half * 2 + s) * ROWS + c, devices, stride=4 * ROWS), :] = results[s]


def short_rows(rows, halo, taps):
    places = lax.broadcasted_iota(jnp.int32, rows.shape, 0)
    once = jnp.where(places < 1, halo[1:2], pltpu.roll(rows, 1, axis=0))
    twice = jnp.where(
        places < 1, halo[0:1], jnp.where(places < 2, halo[1:2], pltpu.roll(rows, 2, axis=0))
    )
    return taps[0:1] * rows + taps[1:2] * once + taps[2:3] * twice


def prepare_kernel(streams, taps, halo, long_filter, cotangent, out):
    rows = streams.shape[1]
    tiles = streams.shape[2] // LANES
    per_tile = LANES // ROWS
    for tile in range(tiles):
        lanes = slice(tile * LANES, (tile + 1) * LANES)
        shorts = [
            short_rows(
                streams[i, :, lanes].astype(jnp.float32), halo[2 * i : 2 * i + 2, lanes], taps[i, :, lanes]
            )
            for i in range(3)
        ]
        gated = shorts[1] * shorts[2]
        carried = cotangent[:, lanes].astype(jnp.float32) * shorts[0]
        half, start = tile // (tiles // 2), tile % (tiles // 2) * per_tile
        for s, series in enumerate((long_filter[:, lanes], gated, carried)):
            turned = jnp.transpose(series).reshape(per_tile, ROWS, rows)
            out[start : start + per_tile, (half * 3 + s) * ROWS : (half * 3 + s + 1) * ROWS, :] = turned


def passed_along(block, axis, distance):
    devices = range(lax.axis_size(axis))
    route = [(i - distance, i) for i in devices if i - distance in devices]
    return lax.ppermute(block, axis, route)


def local(streams, short_taps, long_filter, skip_bias, norm_gain, cotangent):
    rows, chans = streams.shape[1], streams.shape[2]
    devices = lax.axis_size("seq")
    rim = short_taps.shape[1] - 1
    halo = passed_along(streams[:, rows - rim :, :].astype(jnp.float32), "seq", 1)
    params = pltpu.CompilerParams(vmem_limit_bytes=40 << 20)
    sent = pl.pallas_call(
        prepare_kernel,
        out_shape=jax.ShapeDtypeStruct((devices, 6 * ROWS, rows), jnp.float32),
        in_specs=[WHOLE] * 5,
        out_specs=WHOLE,
        compiler_params=params,
    )(streams, short_taps, halo.reshape(3 * rim, chans), long_filter, cotangent)
    got = lax.all_to_all(sent, "seq", split_axis=0, concat_axis=0, tiled=True)
    returned = pl.pallas_call(
        functools.partial(spectral_kernel, devices),
        out_shape=jax.ShapeDtypeStruct((devices * 4 * ROWS, rows), jnp.float32),
        in_specs=[WHOLE] * 6,
        out_specs=WHOLE,
        compiler_params=params,
    )(got.reshape(devices * 6 * ROWS, rows), *tables(devices, rows))
    back = lax.all_to_all(
        returned.reshape(devices, 4 * ROWS, rows), "seq", split_axis=0, concat_axis=0, tiled=True
    )
    back = back.reshape(devices, 2, 2, ROWS, rows).transpose(2, 4, 1, 0, 3).reshape(2, rows, chans)
    convolved, correlated = back[0], back[1]

    widened = streams.astype(jnp.float32)
    extended = jnp.concatenate([halo, widened], axis=1)
    shorts = sum(
        short_taps[:, j, None, :] * extended[:, rim - j : rim - j + rows, :] for j in range(rim + 1)
    )
    short_q, short_k, short_v = (shorts[0], shorts[1], shorts[2])
    gated = short_k * short_v
    cot_wide = cotangent.astype(jnp.float32)
    carried = cot_wide * short_q
    direct = convolved + skip_bias * gated
    mixed = short_q * direct
    square_sum = lax.psum(jnp.sum(mixed * mixed, axis=1), "ch")
    scaling = lax.rsqrt(square_sum[:, None] / (chans * lax.axis_size("ch")) + 1e-06)
    normed = (mixed * scaling * norm_gain).astype(jnp.bfloat16)
    gated_grad = correlated + skip_bias * carried
    short_grad = jnp.stack([cot_wide * direct, gated_grad * short_v, gated_grad * short_k])
    following = passed_along(short_grad[:, :rim, :], "seq", -1)
    grad_ext = jnp.concatenate([short_grad, following], axis=1)
    grads = sum(short_taps[:, j, None, :] * grad_ext[:, j : j + rows, :] for j in range(rim + 1))
    return (normed, grads.astype(jnp.bfloat16))


def solution(mesh):
    placed = (
        P(None, "seq", "ch"),
        P(None, None, "ch"),
        P("seq", "ch"),
        P("ch"),
        P("ch"),
        P("seq", "ch"),
    )
    return jax.shard_map(
        local,
        mesh=mesh,
        in_specs=placed,
        out_specs=(P("seq", "ch"), P(None, "seq", "ch")),
        check_vma=False,
    )
```

time: 462 us -> 139 us (0.30)
  blocking collectives: 190 us -> 60.9 us
  waiting for transfers between devices: 133 us -> 20.6 us
  matrix products: 46.8 us -> 0 us
  local copies, waits for them, and re-layouts: 41.5 us -> 14.2 us
  Pallas kernels: 0 us -> 12.9 us
  starting transfers between devices: 27.5 us -> 16.7 us
  other arithmetic: 17.8 us -> 12.1 us
    all_to_all x2 -> x1, blocking collectives: 181 us -> 52.4 us  [local(): got = lax.all_to_all(sent, 'seq', split_axis=0, concat_axis=0, tiled=True)]
    all_to_all x2 -> x1, waiting for transfers between devices: 133 us -> 19.2 us  [local(): lax.all_to_all(returned.reshape(devices, 4 * ROWS, rows), 'seq', split_ax...]
    dot_general x8 -> x0, matrix products: 46.8 us -> none  [the longest x1 9.37 us: spread_forward(): second = jnp.einsum('jb,bksc->jksc', sin_b, swapped, precision=EXACTNESS)]
    all_to_all x3 -> x0, local copies, waits for them, and re-layouts: 17.3 us -> none  [swap_blocks(): lax.all_to_all(blocks, 'seq', split_axis=1, concat_axis=0, tiled=True)]
    concatenate x2 -> x0, local copies, waits for them, and re-layouts: 15.8 us -> none  [the longest x1 10.3 us: spread_forward(): jnp.concatenate([real_part * turn_cos - imag_part * turn_sin, real_part *...]
    pallas_call x0 -> x2, Pallas kernels: none -> 12.9 us  [the longest x1 12.3 us: local(): pl.pallas_call(functools.partial(spectral_kernel, devices), out_shape=jax...]
    all_to_all x2 -> x1, starting transfers between devices: 19.6 us -> 6.78 us  [local(): lax.all_to_all(returned.reshape(devices, 4 * ROWS, rows), 'seq', split_ax...]
    unnamed x19 -> x36, local copies, waits for them, and re-layouts: 1.94 us -> 8.7 us
  transfers between devices with their start and end apart: 4 -> 3, of which waited for: 2 -> 3; matrix products, arithmetic and copies ran while one was open for 1% -> 8% of each run, Pallas kernels for 0% -> 0%
where the time goes in v1:
time: 139 us; the launch traced here: 138 us
  blocking collectives  60.9 us (44%)
  waiting for transfers between devices  20.6 us (15%)
  starting transfers between devices  16.7 us (12%)
  local copies, waits for them, and re-layouts  14.2 us (10%)
  Pallas kernels  12.9 us (9%)
  other arithmetic  12.1 us (9%)
    all_to_all x1, blocking collectives, local(): got = lax.all_to_all(sent, 'seq', split_axis=0, concat_axis=0, tiled=True)  52.4 us
    all_to_all x1, waiting for transfers between devices, local(): lax.all_to_all(returned.reshape(devices, 4 * ROWS, rows), 'seq', split_ax...  19.2 us
    pallas_call x1, Pallas kernels, local(): pl.pallas_call(functools.partial(spectral_kernel, devices), out_shape=jax...  12.3 us
    ppermute x2, starting transfers between devices, passed_along(): return lax.ppermute(block, axis, route)  9.88 us
    unnamed x36, local copies, waits for them, and re-layouts  8.7 us
    psum x1, blocking collectives, local(): square_sum = lax.psum(jnp.sum(mixed * mixed, axis=1), 'ch')  8.46 us
    all_to_all x1, starting transfers between devices, local(): lax.all_to_all(returned.reshape(devices, 4 * ROWS, rows), 'seq', split_ax...  6.78 us
    add x1, other arithmetic, local(): sum((short_taps[:, j, None, :] * extended[:, rim - j:rim - j + rows, :] f...  4.38 us
  transfers between devices with their start and end apart: 3, of which 3 were waited for; matrix products, arithmetic and copies ran while one was open for 8% of the time, Pallas kernels for 0%

profile of v1, /device:TPU:1, one launch (start us, length us, event | category | flops | bytes accessed | tf_op | source)
XLA Modules:
  0.0 138.1 jit_solution(9511766472826096947)
XLA Ops:
  0.6 0.8 slice_convert_fusion
  1.4 4.6 %collective-permute-start = (f32[3,2,1024]{2,1,0:T(2,128)S(1)}, f32[3,2,1024]{2,1,0:T(2,128)S(1)}, u32[]{:S(2)}, u32[]{:S(2)}) collective-permute-start(f32[3,2,1024]{2,1,0:T(2,128)S(1)} %slice_convert_fusion), channel_id=1, source_target_pairs={{0,4},{4,8},{8,12},{12,16},{16,20},{20,24},{24,28},{28,32},{32,36}... | collective-permute-start | bytes 73736 | tf_op jit(solution)/shard_map/ppermute | solution.py:146
  6.0 0.9 collective-permute-done
  7.0 1.1 copy-done
  8.1 0.9 copy-done.2
  9.1 1.0 copy-done.4
  10.1 0.8 copy-done.7
  10.9 0.6 shard_map.122
  11.6 52.4 %all_to_all.10 = f32[64,48,128]{2,1,0:T(8,128)S(1)} all-to-all(f32[64,48,128]{2,1,0:T(8,128)S(1)} %shard_map.122), channel_id=1, replica_groups=mesh['seq'=64,'ch'=4] {'seq'}, dimensions={0} | all-to-all | bytes 3145728 | tf_op jit(solution)/shard_map/all_to_all | solution.py:162
  64.0 12.3 %shard_map.123 = f32[2048,128]{1,0:T(8,128)} custom-call(f32[3072,128]{1,0:T(8,128)S(1)} %bitcast.56, bf16[128,192]{1,0:T(8,128)(2,1)S(1)} %copy-done.10, f32[2,64,128]{2,1,0:T(8,128)S(1)} %copy-done.9, bf16[768,256]{1,0:T(8,128)(2,1)S(1)} %copy-done.6, bf16[768,256]{1,0:T(8,128)(2,1)S(1)} %copy-done.5, bf16[64,384]{1,0:T(8,128)(2,1)S(1)} %copy-done.11), custom_call_target="tpu_custom_call" | custom-call | tf_op jit(solution)/shard_map/pallas_call | solution.py:163
  76.3 6.8 %all-to-all-start.1 = ((f32[64,32,128]{2,1,0:T(8,128)}), f32[64,32,128]{2,1,0:T(8,128)}, u32[]{:S(2)}, u32[]{:S(2)}) async-start(f32[64,32,128]{2,1,0:T(8,128)} %bitcast.2), calls=%async_computation.1 | async-start | bytes 2097152 | tf_op jit(solution)/shard_map/all_to_all | solution.py:170
  83.1 0.2 copy.31
  83.3 1.2 copy.28
  84.5 1.2 convert_element_type.15
  85.8 1.7 %copy.29 = f32[3,2,1024]{1,2,0:T(8,128)} copy(f32[3,2,1024]{2,1,0:T(2,128)S(1)} %collective-permute-done) | data formatting | bytes 49152 | tf_op jit(solution)/shard_map/ppermute | solution.py:146
  87.5 4.4 %fusion.3 = f32[3,128,1024]{1,2,0:T(8,128)S(1)} fusion(f32[3,2,1024]{1,2,0:T(8,128)} %copy.29, f32[3,128,1024]{1,2,0:T(8,128)S(1)} %convert_element_type.15, f32[3,1024]{1,0:T(4,128)S(1)} %get-tuple-element.19, f32[3,1024]{1,0:T(4,128)S(1)} %get-tuple-element.20, f32[3,1024]{1,0:T(4,128)S(1)} %bitcast.58), kind=kLoop, calls=%fused_computation.6 | loop fusion | flops 2752512 | bytes 3207168 | tf_op jit(solution)/shard_map/add | solution.py:178
  91.8 19.2 %all-to-all-done.1 = f32[64,32,128]{2,1,0:T(8,128)} async-done(((f32[64,32,128]{2,1,0:T(8,128)}), f32[64,32,128]{2,1,0:T(8,128)}, u32[]{:S(2)}, u32[]{:S(2)}) %all-to-all-start.1) | async-done | bytes 1048608 | tf_op jit(solution)/shard_map/all_to_all | solution.py:170
  111.0 1.3 fusion.12
  112.4 0.6 copy-done.14
  113.0 0.3 multiply_bitcast_fusion.1
  113.3 0.8 copy-done.12
  114.3 8.5 %psum.7 = f32[128]{0:T(128)S(1)} all-reduce(f32[128]{0:T(128)S(1)} %multiply_reduce_fusion), channel_id=1, replica_groups=mesh['seq'=64,'ch'=4] {'ch'}, use_global_device_ids=true, to_apply=%region_1.0 | all-reduce | flops 128 | bytes 1024 | tf_op jit(solution)/shard_map/psum | solution.py:187
  122.7 1.3 pad_maximum_fusion.2
  124.0 1.9 %copy.33 = f32[3,2,1024]{2,1,0:T(2,128)S(1)} copy(f32[3,2,1024]{1,2,0:T(8,128)} %bitcast.57) | data formatting | bytes 49152 | tf_op jit(solution)/shard_map/slice | solution.py:192
  125.9 5.3 %collective-permute-start.1 = (f32[3,2,1024]{2,1,0:T(2,128)S(1)}, f32[3,2,1024]{2,1,0:T(2,128)S(1)}, u32[]{:S(2)}, u32[]{:S(2)}) collective-permute-start(f32[3,2,1024]{2,1,0:T(2,128)S(1)} %copy.33), channel_id=1, source_target_pairs={{4,0},{8,4},{12,8},{16,12},{20,16},{24,20},{28,24},{32,28},{36,32}... | collective-permute-start | bytes 73736 | tf_op jit(solution)/shard_map/ppermute | solution.py:146
  131.2 1.2 multiply_convert_fusion
  132.5 0.9 copy.35
  133.3 0.5 collective-permute-done.1
  133.8 0.5 copy.34
  134.3 0.2 pad_maximum_fusion
  134.5 2.4 %fusion.5 = bf16[3,128,1024]{1,2,0:T(8,128)(2,1)S(1)} fusion(f32[3,130,1024]{1,2,0:T(8,128)S(1)} %pad_maximum_fusion, f32[3,1024]{1,0:T(4,128)S(1)} %get-tuple-element.19, f32[3,1024]{1,0:T(4,128)S(1)} %get-tuple-element.20, f32[3,1024]{1,0:T(4,128)S(1)} %bitcast.59, f32[1,128,1024]{1,2,0:T(8,128)S(1)} %get-tuple-element.11, ...), kind=kLoop, calls=%fused_computation.9 | loop fusion | flops 3145728 | bytes 5541888 | tf_op jit(solution)/shard_map/convert_element_type | solution.py:195
  136.9 1.2 copy.36
  (32 shorter events, 0.4 us)
Async XLA Ops:
  1.4 5.5 %collective-permute-start = (f32[3,2,1024]{2,1,0:T(2,128)S(1)}, f32[3,2,1024]{2,1,0:T(2,128)S(1)}, u32[]{:S(2)}, u32[]{:S(2)}) collective-permute-start(f32[3,2,1024]{2,1,0:T(2,128)S(1)} %slice_convert_fusion), channel_id=1, source_target_pairs={{0,4},{4,8},{8,12},{12,16},{16,20},{20,24},{24,28},{28,32},{32,36}... | collective-permute-start | bytes 73736 | tf_op jit(solution)/shard_map/ppermute | solution.py:146
  7.0 1.1 copy-start
  8.1 0.9 copy-start.2
  9.1 1.0 copy-start.4
  10.1 0.8 copy-start.7
  11.6 52.5 %copy-start.5 = (bf16[768,256]{1,0:T(8,128)(2,1)S(1)}, bf16[768,256]{1,0:T(8,128)(2,1)}, u32[]{:S(2)}) copy-start(bf16[768,256]{1,0:T(8,128)(2,1)} %constant.20.clone.backward) | copy-start | bytes 1179652
  11.6 52.4 %copy-start.6 = (bf16[768,256]{1,0:T(8,128)(2,1)S(1)}, bf16[768,256]{1,0:T(8,128)(2,1)}, u32[]{:S(2)}) copy-start(bf16[768,256]{1,0:T(8,128)(2,1)} %constant.19.clone.forward) | copy-start | bytes 1179652
  11.6 52.4 %copy-start.9 = (f32[2,64,128]{2,1,0:T(8,128)S(1)}, f32[2,64,128]{2,1,0:T(8,128)}, u32[]{:S(2)}) copy-start(f32[2,64,128]{2,1,0:T(8,128)} %constant.18.clone.turn) | copy-start | bytes 196612
  11.6 52.4 %copy-start.10 = (bf16[128,192]{1,0:T(8,128)(2,1)S(1)}, bf16[128,192]{1,0:T(8,128)(2,1)}, u32[]{:S(2)}) copy-start(bf16[128,192]{1,0:T(8,128)(2,1)} %constant.17.clone.first) | copy-start | bytes 147460
  11.6 52.4 %copy-start.11 = (bf16[64,384]{1,0:T(8,128)(2,1)S(1)}, bf16[64,384]{1,0:T(8,128)(2,1)}, u32[]{:S(2)}) copy-start(bf16[64,384]{1,0:T(8,128)(2,1)} %constant.21.clone.last) | copy-start | bytes 147460
  76.3 6.8 %copy-start.3 = (bf16[128,1024]{1,0:T(8,128)(2,1)S(1)}, bf16[128,1024]{1,0:T(8,128)(2,1)}, u32[]{:S(2)}) copy-start(bf16[128,1024]{1,0:T(8,128)(2,1)} %cotangent.1) | copy-start | bytes 786436
  76.3 7.0 %copy-start.1 = (bf16[3,128,1024]{2,1,0:T(8,128)(2,1)S(1)}, bf16[3,128,1024]{2,1,0:T(8,128)(2,1)}, u32[]{:S(2)}) copy-start(bf16[3,128,1024]{2,1,0:T(8,128)(2,1)} %streams.1) | copy-start | bytes 2359300
  76.3 34.7 %all-to-all-start.1 = ((f32[64,32,128]{2,1,0:T(8,128)}), f32[64,32,128]{2,1,0:T(8,128)}, u32[]{:S(2)}, u32[]{:S(2)}) async-start(f32[64,32,128]{2,1,0:T(8,128)} %bitcast.2), calls=%async_computation.1 | async-start | bytes 2097152 | tf_op jit(solution)/shard_map/all_to_all | solution.py:170
  83.1 1.4 copy-start.8
  112.3 0.7 copy-start.14
  113.3 0.8 copy-start.12
  124.0 7.2 %copy-start.13 = (f32[1024]{0:T(1024)S(1)}, f32[1024]{0:T(1024)}, u32[]{:S(2)}) copy-start(f32[1024]{0:T(1024)} %param.15) | copy-start | bytes 12292
  125.9 7.9 %collective-permute-start.1 = (f32[3,2,1024]{2,1,0:T(2,128)S(1)}, f32[3,2,1024]{2,1,0:T(2,128)S(1)}, u32[]{:S(2)}, u32[]{:S(2)}) collective-permute-start(f32[3,2,1024]{2,1,0:T(2,128)S(1)} %copy.33), channel_id=1, source_target_pairs={{4,0},{8,4},{12,8},{16,12},{20,16},{24,20},{28,24},{32,28},{36,32}... | collective-permute-start | bytes 73736 | tf_op jit(solution)/shard_map/ppermute | solution.py:146

commit v2 on v1

v2 whole, which is shorter than its diff:
```python
import functools

import jax
import jax.numpy as jnp
import ml_dtypes
import numpy as np
from jax import lax
from jax.experimental import pallas as pl
from jax.experimental.pallas import tpu as pltpu
from jax.sharding import PartitionSpec as P

LANES = 128
ROWS = 8
MESH = pl.DeviceIdType.MESH
WHOLE = pl.BlockSpec(memory_space=pltpu.VMEM)
ANYWHERE = pl.BlockSpec(memory_space=pltpu.HBM)


def halves_of(table):
    high = table.astype(ml_dtypes.bfloat16)
    low = (table - high.astype(np.float64)).astype(ml_dtypes.bfloat16)
    return high, low


@functools.lru_cache(None)
def tables(devices, rows):
    length = devices * rows
    outer = np.arange(devices)
    inner = np.arange(rows)
    shifted = outer + 0.25
    angle = 2.0 * np.pi * np.outer(shifted, outer) / devices
    first = np.concatenate([np.cos(angle), -np.sin(angle)], axis=0)
    high, low = halves_of(first)
    first = np.concatenate([high, high, low], axis=1)
    last = np.concatenate([np.cos(angle).T, -np.sin(angle).T], axis=1) / length
    high, low = halves_of(last)
    last = np.concatenate([high, high, low], axis=1)
    turn = 2.0 * np.pi * np.outer(shifted, inner) / length
    turn = np.stack([np.cos(turn), -np.sin(turn)]).astype(np.float32)
    angle = 2.0 * np.pi * (np.outer(inner, inner) % rows) / rows
    cos, sin = np.cos(angle), np.sin(angle)
    high, low = halves_of(np.block([[cos, -sin], [sin, cos]]))
    forward = np.concatenate([high, high, low], axis=0)
    high, low = halves_of(np.block([[cos, sin], [-sin, cos]]))
    backward = np.concatenate([high, high, low], axis=0)
    return first, turn, forward, backward, last


def split(x):
    high = x.astype(jnp.bfloat16)
    low = (x - high.astype(jnp.float32)).astype(jnp.bfloat16)
    return high, low


def stacked_rows(x):
    high, low = split(x)
    return jnp.concatenate([high, low, high], axis=0)


def stacked_lanes(x):
    high, low = split(x)
    return jnp.concatenate([high, low, high], axis=1)


def product(a, b):
    return jnp.dot(a, b, preferred_element_type=jnp.float32)


def both_products(filtered, gated, carried, first, turn, forward, backward, last):
    devices = filtered.shape[0]
    turn_re, turn_im = turn[0], turn[1]
    joined = jnp.concatenate([filtered, gated, carried], axis=1)
    opened = product(first[...], stacked_rows(joined))
    parts = []
    for i in range(3):
        re = opened[:devices, i * LANES : (i + 1) * LANES]
        im = opened[devices:, i * LANES : (i + 1) * LANES]
        parts.append(
            jnp.concatenate([re * turn_re - im * turn_im, re * turn_im + im * turn_re], axis=1)
        )
    spectra = product(stacked_lanes(jnp.concatenate(parts, axis=0)), forward[...])
    filter_re, filter_im = spectra[:devices, :LANES], spectra[:devices, LANES:]
    gated_re, gated_im = spectra[devices : 2 * devices, :LANES], spectra[devices : 2 * devices, LANES:]
    carry_re, carry_im = spectra[2 * devices :, :LANES], spectra[2 * devices :, LANES:]
    forth = jnp.concatenate(
        [filter_re * gated_re - filter_im * gated_im, filter_re * gated_im + filter_im * gated_re],
        axis=1,
    )
    back = jnp.concatenate(
        [filter_re * carry_re + filter_im * carry_im, filter_re * carry_im - filter_im * carry_re],
        axis=1,
    )
    closed = product(stacked_lanes(jnp.concatenate([forth, back], axis=0)), backward[...])
    turned = []
    for i in range(2):
        re = closed[i * devices : (i + 1) * devices, :LANES]
        im = closed[i * devices : (i + 1) * devices, LANES:]
        turned.append(
            jnp.concatenate([re * turn_re + im * turn_im, im * turn_re - re * turn_im], axis=0)
        )
    result = product(last[...], stacked_rows(jnp.concatenate(turned, axis=1)))
    return result[:, :LANES], result[:, LANES:]


def short_rows(rows, halo, taps):
    places = lax.broadcasted_iota(jnp.int32, rows.shape, 0)
    once = jnp.where(places < 1, halo[1:2], pltpu.roll(rows, 1, axis=0))
    twice = jnp.where(
        places < 1, halo[0:1], jnp.where(places < 2, halo[1:2], pltpu.roll(rows, 2, axis=0))
    )
    return taps[0:1] * rows + taps[1:2] * once + taps[2:3] * twice


def block_at(ref, index, rows):
    return ref.at[pl.ds(pl.multiple_of(index * rows, rows), rows)]


def await_bytes(ref, semaphore):
    pltpu.make_async_copy(ref, ref, semaphore).wait()


def operator_kernel(
    devices,
    groups,
    streams_in,
    taps_in,
    filter_in,
    bias_in,
    gain_in,
    cot_in,
    first_in,
    turn_in,
    forward_in,
    backward_in,
    last_in,
    normed,
    grads,
    streams,
    taps,
    filters,
    bias,
    gain,
    cot,
    first,
    turn,
    forward,
    backward,
    last,
    sent,
    got,
    shorts,
    mixed,
    edge,
    rim_sent,
    rim_got,
    squares_sent,
    squares_got,
    load_sems,
    send_sems,
    recv_sems,
    own_sems,
    small_send,
    small_recv,
):
    me = lax.axis_index("seq")
    group = lax.axis_index("ch")
    rows, chans = streams.shape[1], streams.shape[2]
    tiles = chans // LANES
    per_tile = LANES // ROWS
    block = 2 * ROWS
    barrier = pltpu.get_barrier_semaphore()

    def greet(i, carry):
        pl.semaphore_signal(
            barrier, 1, device_id={"seq": (me + i) % devices}, device_id_type=MESH
        )
        return carry

    lax.fori_loop(1, devices, greet, 0)
    for i in range(1, groups):
        pl.semaphore_signal(
            barrier, 1, device_id={"ch": (group + i) % groups}, device_id_type=MESH
        )

    loads = []
    pairs = (
        (filter_in, filters),
        (streams_in, streams),
        (taps_in, taps),
        (cot_in, cot),
        (first_in, first),
        (turn_in, turn),
        (forward_in, forward),
        (backward_in, backward),
        (last_in, last),
        (bias_in, bias),
        (gain_in, gain),
    )
    for i, (source, target) in enumerate(pairs):
        load = pltpu.make_async_copy(source, target, load_sems.at[i])
        load.start()
        loads.append(load)

    def lanes_of(tile):
        return slice(tile * LANES, (tile + 1) * LANES)

    def put(phase, part, tile, series):
        start = tile % (tiles // 2) * per_tile
        turned = jnp.transpose(series).reshape(per_tile, ROWS, rows)
        for i in range(per_tile):
            at = (start + i) * block + part * ROWS
            sent[phase, at : at + ROWS, :] = turned[i]

    def exchange(phase):
        own = pltpu.make_async_copy(
            block_at(sent.at[phase], me, block),
            block_at(got.at[phase], me, block),
            own_sems.at[phase],
        )
        own.start()

        def go(i, carry):
            peer = (me + i) % devices
            pltpu.make_async_remote_copy(
                src_ref=block_at(sent.at[phase], peer, block),
                dst_ref=block_at(got.at[phase], me, block),
                send_sem=send_sems.at[phase],
                recv_sem=recv_sems.at[phase],
                device_id={"seq": peer},
                device_id_type=MESH,
            ).start()
            return carry

        lax.fori_loop(1, devices, go, 0)
        return own

    def others(ref, phase):
        return ref.at[phase, pl.ds(0, (devices - 1) * block)]

    def arrive(phase, own):
        own.wait()
        await_bytes(others(got, phase), recv_sems.at[phase])

    loads[0].wait()
    for tile in range(tiles):
        put(0, tile // (tiles // 2), tile, filters[:, lanes_of(tile)])
    loads[1].wait()
    loads[2].wait()
    loads[3].wait()
    rim_sent[0] = jnp.zeros((ROWS, chans), jnp.float32)
    for i in range(3):
        rim_sent[0, 2 * i : 2 * i + 2, :] = streams[i, rows - 2 : rows, :].astype(jnp.float32)
    pl.semaphore_wait(barrier, devices + groups - 2)

    def rim_copy(which, peer):
        return pltpu.make_async_remote_copy(
            src_ref=rim_sent.at[which],
            dst_ref=rim_got.at[which],
            send_sem=small_send.at[which],
            recv_sem=small_recv.at[which],
            device_id={"seq": peer},
            device_id_type=MESH,
        )

    halo_copy = rim_copy(0, (me + 1) % devices)
    halo_copy.start()
    owns = [exchange(0)]
    halo_copy.wait()
    for half in range(2):
        for tile in range(half * tiles // 2, (half + 1) * tiles // 2):
            lanes = lanes_of(tile)
            halo = jnp.where(me > 0, rim_got[0, :, lanes], 0.0)
            short = [
                short_rows(
                    streams[i, :, lanes].astype(jnp.float32), halo[2 * i : 2 * i + 2], taps[i, :, lanes]
                )
                for i in range(3)
            ]
            for i in range(3):
                shorts[i, :, lanes] = short[i]
            put(1 + half, 0, tile, short[1] * short[2])
            put(1 + half, 1, tile, cot[:, lanes].astype(jnp.float32) * short[0])
        owns.append(exchange(1 + half))

    for load in loads[4:]:
        load.wait()
    arrive(0, owns[0])
    for half in range(2):
        arrive(1 + half, owns[1 + half])
        for c in range(ROWS):
            taken = [
                got[0, pl.ds(half * ROWS + c, devices, stride=block), :],
                got[1 + half, pl.ds(c, devices, stride=block), :],
                got[1 + half, pl.ds(ROWS + c, devices, stride=block), :],
            ]
            results = both_products(*taken, first, turn, forward, backward, last)
            for s in range(2):
                sent[3 + half, pl.ds(s * ROWS + c, devices, stride=block), :] = results[s]
        owns.append(exchange(3 + half))

    places = lax.broadcasted_iota(jnp.int32, (rows, LANES), 0)
    rim_sent[1] = jnp.zeros((ROWS, chans), jnp.float32)
    squares = jnp.zeros((rows, LANES), jnp.float32)
    tail = edge.shape[1]
    for half in range(2):
        arrive(3 + half, owns[3 + half])
        for tile in range(half * tiles // 2, (half + 1) * tiles // 2):
            lanes = lanes_of(tile)
            start = tile % (tiles // 2) * per_tile
            back = []
            for s in range(2):
                pieces = []
                for i in range(per_tile):
                    at = (start + i) * block + s * ROWS
                    pieces.append(got[3 + half, at : at + ROWS, :])
                back.append(jnp.transpose(jnp.concatenate(pieces, axis=0)))
            short_q, short_k, short_v = (shorts[i, :, lanes] for i in range(3))
            cot_wide = cot[:, lanes].astype(jnp.float32)
            skip = bias[:, lanes]
            direct = back[0] + skip * (short_k * short_v)
            mix = short_q * direct
            mixed[:, lanes] = mix
            squares = squares + mix * mix
            gated_grad = back[1] + skip * (cot_wide * short_q)
            short_grad = (cot_wide * direct, gated_grad * short_v, gated_grad * short_k)
            for i in range(3):
                own = short_grad[i]
                rim_sent[1, 2 * i : 2 * i + 2, lanes] = own[0:2]
                once = jnp.where(places < rows - 1, pltpu.roll(own, rows - 1, axis=0), 0.0)
                twice = jnp.where(places < rows - 2, pltpu.roll(own, rows - 2, axis=0), 0.0)
                grad = (
                    taps[i, 0:1, lanes] * own + taps[i, 1:2, lanes] * once + taps[i, 2:3, lanes] * twice
                )
                grads[i, : rows - tail, lanes] = grad[: rows - tail].astype(jnp.bfloat16)
                edge[i, :, lanes] = grad[rows - tail :]

    rim_back = rim_copy(1, (me + devices - 1) % devices)
    rim_back.start()
    total = jnp.sum(jnp.transpose(squares), axis=0, keepdims=True)
    squares_sent[...] = jnp.broadcast_to(total, squares_sent.shape)
    copies = []
    for i in range(1, groups):
        copy = pltpu.make_async_remote_copy(
            src_ref=squares_sent,
            dst_ref=squares_got.at[i - 1],
            send_sem=small_send.at[1 + i],
            recv_sem=small_recv.at[1 + i],
            device_id={"ch": (group + i) % groups},
            device_id_type=MESH,
        )
        copy.start()
        copies.append(copy)
    for copy in copies:
        copy.wait()
    for i in range(1, groups):
        total = total + squares_got[i - 1, 0:1, :]
    scaling = lax.rsqrt(total / (chans * groups) + 1e-06)
    scaling = jnp.transpose(jnp.broadcast_to(scaling, (LANES, rows)))
    for tile in range(tiles):
        lanes = lanes_of(tile)
        normed[:, lanes] = (mixed[:, lanes] * scaling * gain[:, lanes]).astype(jnp.bfloat16)
    rim_back.wait()
    last_places = lax.broadcasted_iota(jnp.int32, (tail, LANES), 0)
    for tile in range(tiles):
        lanes = lanes_of(tile)
        halo = jnp.where(me < devices - 1, rim_got[1, :, lanes], 0.0)
        for i in range(3):
            near, far = halo[2 * i : 2 * i + 1], halo[2 * i + 1 : 2 * i + 2]
            second, third = taps[i, 1:2, lanes], taps[i, 2:3, lanes]
            more = jnp.where(
                last_places == tail - 1,
                second * near + third * far,
                jnp.where(last_places == tail - 2, third * near, 0.0),
            )
            grads[i, rows - tail :, lanes] = (edge[i, :, lanes] + more).astype(jnp.bfloat16)
    for phase in range(5):
        await_bytes(others(sent, phase), send_sems.at[phase])


def local(streams, short_taps, long_filter, skip_bias, norm_gain, cotangent):
    rows, chans = streams.shape[1], streams.shape[2]
    devices, groups = lax.axis_size("seq"), lax.axis_size("ch")
    parts = tables(devices, rows)
    operands = (
        streams,
        short_taps,
        long_filter,
        skip_bias.reshape(1, chans),
        norm_gain.reshape(1, chans),
        cotangent,
    ) + tuple(jnp.asarray(part) for part in parts)
    vmem = [pltpu.VMEM(operand.shape, operand.dtype) for operand in operands]
    tail = 2 * ROWS
    exchanged = (5, devices * 2 * ROWS, rows)
    return pl.pallas_call(
        functools.partial(operator_kernel, devices, groups),
        out_shape=(
            jax.ShapeDtypeStruct((rows, chans), jnp.bfloat16),
            jax.ShapeDtypeStruct(streams.shape, jnp.bfloat16),
        ),
        in_specs=[ANYWHERE] * len(operands),
        out_specs=(WHOLE, WHOLE),
        scratch_shapes=vmem
        + [
            pltpu.VMEM(exchanged, jnp.float32),
            pltpu.VMEM(exchanged, jnp.float32),
            pltpu.VMEM(streams.shape, jnp.float32),
            pltpu.VMEM((rows, chans), jnp.float32),
            pltpu.VMEM((3, tail, chans), jnp.float32),
            pltpu.VMEM((2, ROWS, chans), jnp.float32),
            pltpu.VMEM((2, ROWS, chans), jnp.float32),
            pltpu.VMEM((ROWS, rows), jnp.float32),
            pltpu.VMEM((groups - 1, ROWS, rows), jnp.float32),
            pltpu.SemaphoreType.DMA((len(operands),)),
            pltpu.SemaphoreType.DMA((5,)),
            pltpu.SemaphoreType.DMA((5,)),
            pltpu.SemaphoreType.DMA((5,)),
            pltpu.SemaphoreType.DMA((1 + groups,)),
            pltpu.SemaphoreType.DMA((1 + groups,)),
        ],
        compiler_params=pltpu.CompilerParams(
            collective_id=0, has_side_effects=True, vmem_limit_bytes=62 << 20
        ),
    )(*operands)


def solution(mesh):
    placed = (
        P(None, "seq", "ch"),
        P(None, None, "ch"),
        P("seq", "ch"),
        P("ch"),
        P("ch"),
        P("seq", "ch"),
    )
    return jax.shard_map(
        local,
        mesh=mesh,
        in_specs=placed,
        out_specs=(P("seq", "ch"), P(None, "seq", "ch")),
        check_vma=False,
    )
```

time: 139 us -> 81.3 us (0.58)
  Pallas kernels: 12.9 us -> 76.5 us
  blocking collectives: 60.9 us -> 0 us
  waiting for transfers between devices: 20.6 us -> 0 us
  starting transfers between devices: 16.7 us -> 0 us
  other arithmetic: 12.1 us -> 0 us
  local copies, waits for them, and re-layouts: 14.2 us -> 3.73 us
    pallas_call x2 -> x1, Pallas kernels: 12.9 us -> 76.5 us  [local(): pl.pallas_call(functools.partial(operator_kernel, devices, groups), out_s...]
    all_to_all x1 -> x0, blocking collectives: 52.4 us -> none  [local(): got = lax.all_to_all(sent, 'seq', split_axis=0, concat_axis=0, tiled=True)]
    all_to_all x1 -> x0, waiting for transfers between devices: 19.2 us -> none  [local(): lax.all_to_all(returned.reshape(devices, 4 * ROWS, rows), 'seq', split_ax...]
    ppermute x2 -> x0, starting transfers between devices: 9.88 us -> none  [passed_along(): return lax.ppermute(block, axis, route)]
    psum x1 -> x0, blocking collectives: 8.46 us -> none  [local(): square_sum = lax.psum(jnp.sum(mixed * mixed, axis=1), 'ch')]
    all_to_all x1 -> x0, starting transfers between devices: 6.78 us -> none  [local(): lax.all_to_all(returned.reshape(devices, 4 * ROWS, rows), 'seq', split_ax...]
    convert_element_type x4 -> x0, other arithmetic: 5.65 us -> none  [the longest x1 2.36 us: local(): return (normed, grads.astype(jnp.bfloat16))]
    unnamed x36 -> x2, local copies, waits for them, and re-layouts: 8.7 us -> 3.73 us
  transfers between devices with their start and end apart: 3 -> 0, of which waited for: 3 -> 0; matrix products, arithmetic and copies ran while one was open for 8% -> 0% of each run, Pallas kernels for 0% -> 0%
where the time goes in v2:
time: 81.3 us; the launch traced here: 80.9 us
  Pallas kernels  76.5 us (94%)
  local copies, waits for them, and re-layouts  3.73 us (5%)
    pallas_call x1, Pallas kernels, local(): pl.pallas_call(functools.partial(operator_kernel, devices, groups), out_s...  76.5 us
    unnamed x2, local copies, waits for them, and re-layouts  3.73 us

profile of v2, /device:TPU:1, one launch (start us, length us, event | category | flops | bytes accessed | tf_op | source)
XLA Modules:
  0.0 80.9 jit_solution(9774692589546090869)
XLA Ops:
  0.6 76.5 %shard_map.122 = (bf16[128,1024]{1,0:T(8,128)(2,1)}, bf16[3,128,1024]{2,1,0:T(8,128)(2,1)}) custom-call(bf16[3,128,1024]{2,1,0:T(8,128)(2,1)} %streams_in.1, f32[3,3,1024]{2,1,0:T(4,128)} %taps_in.1, f32[128,1024]{1,0:T(8,128)} %filter_in.1, f32[1,1024]{1,0:T(1,128)} %bitcast.2, f32[1,1024]{1,0:T(1,128)} %bitcast.3, bf16[128,1024]{1,0:T(8,128)(2,1)} %cot_in.1, ...), custom_call_target="tpu_custom_call" | custom-call | tf_op jit(solution)/shard_map/pallas_call | solution.py:395
  77.2 1.7 %copy.15 = bf16[128,1024]{1,0:T(8,128)(2,1)} copy(bf16[128,1024]{1,0:T(8,128)(2,1)} %get-tuple-element.4) | data formatting | bytes 524288
  78.9 2.1 %copy.16 = bf16[3,128,1024]{2,1,0:T(8,128)(2,1)} copy(bf16[3,128,1024]{2,1,0:T(8,128)(2,1)} %get-tuple-element.5) | data formatting | bytes 1572864

commit v3 on v2

--- a/solution.py
+++ b/solution.py
@@ -419,9 +419,9 @@
             pltpu.SemaphoreType.DMA((1 + groups,)),
         ],
         compiler_params=pltpu.CompilerParams(
-            collective_id=0, has_side_effects=True, vmem_limit_bytes=62 << 20
+            collective_id=0, has_side_effects=True, vmem_limit_bytes=48 << 20
         ),
-    )(*operands)
+    )(*(pltpu.with_memory_space_constraint(o, pltpu.HBM) for o in operands))
 
 
 def solution(mesh):

time: 81.3 us -> 78.1 us (0.961)
  local copies, waits for them, and re-layouts: 3.73 us -> 1.58 us
  Pallas kernels: 76.5 us -> 75.5 us
    unnamed x2, local copies, waits for them, and re-layouts: 3.73 us -> 1.58 us
    pallas_call x1, Pallas kernels: 76.5 us -> 75.5 us  [local(): pl.pallas_call(functools.partial(operator_kernel, devices, groups), out_s...]
where the time goes in v3:
time: 78.1 us; the launch traced here: 77.8 us
  Pallas kernels  75.5 us (97%)
  local copies, waits for them, and re-layouts  1.58 us (2%)
    pallas_call x1, Pallas kernels, local(): pl.pallas_call(functools.partial(operator_kernel, devices, groups), out_s...  75.5 us
    unnamed x2, local copies, waits for them, and re-layouts  1.58 us

profile of v3, /device:TPU:1, one launch (start us, length us, event | category | flops | bytes accessed | tf_op | source)
XLA Modules:
  0.0 77.8 jit_solution(2481245067913802406)
XLA Ops:
  0.6 75.5 %shard_map.122 = (bf16[128,1024]{1,0:T(8,128)(2,1)S(1)}, bf16[3,128,1024]{2,1,0:T(8,128)(2,1)S(1)}) custom-call(bf16[3,128,1024]{2,1,0:T(8,128)(2,1)} %streams_in.1, f32[3,3,1024]{2,1,0:T(4,128)} %taps_in.1, f32[128,1024]{1,0:T(8,128)} %filter_in.1, f32[1,1024]{1,0:T(1,128)} %bitcast.2, f32[1,1024]{1,0:T(1,128)} %bitcast.3, bf16[128,1024]{1,0:T(8,128)(2,1)} %cot_in.1, ...), custom_call_target="tpu_custom_call" | custom-call | tf_op jit(solution)/shard_map/pallas_call | solution.py:395
  76.2 0.7 copy.15
  76.9 0.9 %copy.16 = bf16[3,128,1024]{2,1,0:T(8,128)(2,1)} copy(bf16[3,128,1024]{2,1,0:T(8,128)(2,1)S(1)} %get-tuple-element.5) | data formatting | bytes 1572864

commit v4 on v3

--- a/solution.py
+++ b/solution.py
@@ -11,6 +11,8 @@
 
 LANES = 128
 ROWS = 8
+SLAB = 8
+SLAB_ORDER = (0, 1, 2, 3, 6, 7, 4, 5)
 MESH = pl.DeviceIdType.MESH
 WHOLE = pl.BlockSpec(memory_space=pltpu.VMEM)
 ANYWHERE = pl.BlockSpec(memory_space=pltpu.HBM)
@@ -66,40 +68,50 @@
     return jnp.dot(a, b, preferred_element_type=jnp.float32)
 
 
-def both_products(filtered, gated, carried, first, turn, forward, backward, last):
-    devices = filtered.shape[0]
+def both_products(channels, first, turn, forward, backward, last):
+    devices = channels[0][0].shape[0]
     turn_re, turn_im = turn[0], turn[1]
-    joined = jnp.concatenate([filtered, gated, carried], axis=1)
-    opened = product(first[...], stacked_rows(joined))
+    series = [one for channel in channels for one in channel]
+    opened = product(first[...], jnp.concatenate([stacked_rows(one) for one in series], axis=1))
     parts = []
-    for i in range(3):
+    for i in range(len(series)):
         re = opened[:devices, i * LANES : (i + 1) * LANES]
         im = opened[devices:, i * LANES : (i + 1) * LANES]
         parts.append(
-            jnp.concatenate([re * turn_re - im * turn_im, re * turn_im + im * turn_re], axis=1)
+            stacked_lanes(
+                jnp.concatenate([re * turn_re - im * turn_im, re * turn_im + im * turn_re], axis=1)
+            )
         )
-    spectra = product(stacked_lanes(jnp.concatenate(parts, axis=0)), forward[...])
-    filter_re, filter_im = spectra[:devices, :LANES], spectra[:devices, LANES:]
-    gated_re, gated_im = spectra[devices : 2 * devices, :LANES], spectra[devices : 2 * devices, LANES:]
-    carry_re, carry_im = spectra[2 * devices :, :LANES], spectra[2 * devices :, LANES:]
-    forth = jnp.concatenate(
-        [filter_re * gated_re - filter_im * gated_im, filter_re * gated_im + filter_im * gated_re],
-        axis=1,
-    )
-    back = jnp.concatenate(
-        [filter_re * carry_re + filter_im * carry_im, filter_re * carry_im - filter_im * carry_re],
-        axis=1,
-    )
-    closed = product(stacked_lanes(jnp.concatenate([forth, back], axis=0)), backward[...])
+    spectra = product(jnp.concatenate(parts, axis=0), forward[...])
+
+    def spectrum(i):
+        piece = spectra[i * devices : (i + 1) * devices]
+        return piece[:, :LANES], piece[:, LANES:]
+
+    parts = []
+    for c in range(len(channels)):
+        filter_re, filter_im = spectrum(3 * c)
+        gated_re, gated_im = spectrum(3 * c + 1)
+        carry_re, carry_im = spectrum(3 * c + 2)
+        forth = (filter_re * gated_re - filter_im * gated_im, filter_re * gated_im + filter_im * gated_re)
+        back = (filter_re * carry_re + filter_im * carry_im, filter_re * carry_im - filter_im * carry_re)
+        parts.append(stacked_lanes(jnp.concatenate(forth, axis=1)))
+        parts.append(stacked_lanes(jnp.concatenate(back, axis=1)))
+    closed = product(jnp.concatenate(parts, axis=0), backward[...])
     turned = []
-    for i in range(2):
+    for i in range(2 * len(channels)):
         re = closed[i * devices : (i + 1) * devices, :LANES]
         im = closed[i * devices : (i + 1) * devices, LANES:]
         turned.append(
-            jnp.concatenate([re * turn_re + im * turn_im, im * turn_re - re * turn_im], axis=0)
+            stacked_rows(
+                jnp.concatenate([re * turn_re + im * turn_im, im * turn_re - re * turn_im], axis=0)
+            )
         )
-    result = product(last[...], stacked_rows(jnp.concatenate(turned, axis=1)))
-    return result[:, :LANES], result[:, LANES:]
+    result = product(last[...], jnp.concatenate(turned, axis=1))
+    return [
+        [result[:, (2 * c + s) * LANES : (2 * c + s + 1) * LANES] for s in range(2)]
+        for c in range(len(channels))
+    ]
 
 
 def short_rows(rows, halo, taps):
@@ -133,7 +145,8 @@
     forward_in,
     backward_in,
     last_in,
-    normed,
+    mixed,
+    scales,
     grads,
     streams,
     taps,
@@ -149,7 +162,6 @@
     sent,
     got,
     shorts,
-    mixed,
     edge,
     rim_sent,
     rim_got,
@@ -159,6 +171,7 @@
     send_sems,
     recv_sems,
     own_sems,
+    slab_sem,
     small_send,
     small_recv,
 ):
@@ -170,13 +183,19 @@
     block = 2 * ROWS
     barrier = pltpu.get_barrier_semaphore()
 
-    def greet(i, carry):
-        pl.semaphore_signal(
-            barrier, 1, device_id={"seq": (me + i) % devices}, device_id_type=MESH
-        )
-        return carry
-
-    lax.fori_loop(1, devices, greet, 0)
+    slabs = devices // SLAB
+    slab, place = me // SLAB, me % SLAB
+
+    def within(i):
+        return slab * SLAB + (place + i) % SLAB
+
+    def across(i):
+        return (slab + i) % slabs * SLAB + place
+
+    for i in range(1, slabs):
+        pl.semaphore_signal(barrier, 1, device_id={"seq": across(i)}, device_id_type=MESH)
+    for i in range(1, SLAB):
+        pl.semaphore_signal(barrier, 1, device_id={"seq": within(i)}, device_id_type=MESH)
     for i in range(1, groups):
         pl.semaphore_signal(
             barrier, 1, device_id={"ch": (group + i) % groups}, device_id_type=MESH
@@ -211,28 +230,50 @@
             at = (start + i) * block + part * ROWS
             sent[phase, at : at + ROWS, :] = turned[i]
 
-    def exchange(phase):
+    def keep(phase):
         own = pltpu.make_async_copy(
             block_at(sent.at[phase], me, block),
             block_at(got.at[phase], me, block),
             own_sems.at[phase],
         )
         own.start()
-
+        return own
+
+    def send(phase, peer):
+        pltpu.make_async_remote_copy(
+            src_ref=block_at(sent.at[phase], peer, block),
+            dst_ref=block_at(got.at[phase], me, block),
+            send_sem=send_sems.at[phase],
+            recv_sem=recv_sems.at[phase],
+            device_id={"seq": peer},
+            device_id_type=MESH,
+        ).start()
+
+    def send_all(phase, peer_of, start, stop):
         def go(i, carry):
-            peer = (me + i) % devices
-            pltpu.make_async_remote_copy(
-                src_ref=block_at(sent.at[phase], peer, block),
-                dst_ref=block_at(got.at[phase], me, block),
-                send_sem=send_sems.at[phase],
-                recv_sem=recv_sems.at[phase],
-                device_id={"seq": peer},
-                device_id_type=MESH,
-            ).start()
+            send(phase, peer_of(i))
             return carry
 
-        lax.fori_loop(1, devices, go, 0)
-        return own
+        lax.fori_loop(start, stop, go, 0)
+
+    def hand_back(phase):
+        for target in SLAB_ORDER:
+
+            def go(i, carry):
+                peer = target * SLAB + (place + i) % SLAB
+
+                @pl.when(peer != me)
+                def _():
+                    send(phase, peer)
+
+                return carry
+
+            lax.fori_loop(0, SLAB, go, 0)
+        return keep(phase)
+
+    def exchange(phase):
+        send_all(phase, lambda i: (me + i) % devices, 1, devices)
+        return keep(phase)
 
     def others(ref, phase):
         return ref.at[phase, pl.ds(0, (devices - 1) * block)]
@@ -250,7 +291,9 @@
     rim_sent[0] = jnp.zeros((ROWS, chans), jnp.float32)
     for i in range(3):
         rim_sent[0, 2 * i : 2 * i + 2, :] = streams[i, rows - 2 : rows, :].astype(jnp.float32)
-    pl.semaphore_wait(barrier, devices + groups - 2)
+    pl.semaphore_wait(barrier, slabs + SLAB + groups - 3)
+    for i in range(1, slabs):
+        pl.semaphore_signal(slab_sem, 1, device_id={"seq": across(i)}, device_id_type=MESH)
 
     def rim_copy(which, peer):
         return pltpu.make_async_remote_copy(
@@ -262,9 +305,18 @@
             device_id_type=MESH,
         )
 
+    send_all(0, across, 1, slabs)
+    send_all(0, within, 1, SLAB)
+    pl.semaphore_wait(slab_sem, slabs - 1)
     halo_copy = rim_copy(0, (me + 1) % devices)
     halo_copy.start()
-    owns = [exchange(0)]
+
+    def elsewhere(i):
+        ahead, beside = i % (slabs - 1) + 1, i // (slabs - 1) + 1
+        return (slab + ahead) % slabs * SLAB + (place + beside) % SLAB
+
+    send_all(0, elsewhere, 0, (slabs - 1) * (SLAB - 1))
+    owns = [keep(0)]
     halo_copy.wait()
     for half in range(2):
         for tile in range(half * tiles // 2, (half + 1) * tiles // 2):
@@ -287,16 +339,19 @@
     arrive(0, owns[0])
     for half in range(2):
         arrive(1 + half, owns[1 + half])
-        for c in range(ROWS):
-            taken = [
+        channels = [
+            [
                 got[0, pl.ds(half * ROWS + c, devices, stride=block), :],
                 got[1 + half, pl.ds(c, devices, stride=block), :],
                 got[1 + half, pl.ds(ROWS + c, devices, stride=block), :],
             ]
-            results = both_products(*taken, first, turn, forward, backward, last)
+            for c in range(ROWS)
+        ]
+        results = both_products(channels, first, turn, forward, backward, last)
+        for c in range(ROWS):
             for s in range(2):
-                sent[3 + half, pl.ds(s * ROWS + c, devices, stride=block), :] = results[s]
-        owns.append(exchange(3 + half))
+                sent[3 + half, pl.ds(s * ROWS + c, devices, stride=block), :] = results[c][s]
+        owns.append(hand_back(4) if half else exchange(3))
 
     places = lax.broadcasted_iota(jnp.int32, (rows, LANES), 0)
     rim_sent[1] = jnp.zeros((ROWS, chans), jnp.float32)
@@ -319,7 +374,7 @@
             skip = bias[:, lanes]
             direct = back[0] + skip * (short_k * short_v)
             mix = short_q * direct
-            mixed[:, lanes] = mix
+            mixed[:, lanes] = mix * gain[:, lanes]
             squares = squares + mix * mix
             gated_grad = back[1] + skip * (cot_wide * short_q)
             short_grad = (cot_wide * direct, gated_grad * short_v, gated_grad * short_k)
@@ -355,10 +410,7 @@
     for i in range(1, groups):
         total = total + squares_got[i - 1, 0:1, :]
     scaling = lax.rsqrt(total / (chans * groups) + 1e-06)
-    scaling = jnp.transpose(jnp.broadcast_to(scaling, (LANES, rows)))
-    for tile in range(tiles):
-        lanes = lanes_of(tile)
-        normed[:, lanes] = (mixed[:, lanes] * scaling * gain[:, lanes]).astype(jnp.bfloat16)
+    scales[...] = jnp.transpose(jnp.broadcast_to(scaling, (LANES, rows)))
     rim_back.wait()
     last_places = lax.broadcasted_iota(jnp.int32, (tail, LANES), 0)
     for tile in range(tiles):
@@ -377,6 +429,19 @@
         await_bytes(others(sent, phase), send_sems.at[phase])
 
 
+def closing_kernel(mixed, scales, grads, normed_out, grads_out, normed, sems):
+    grads_copy = pltpu.make_async_copy(grads, grads_out, sems.at[0])
+    grads_copy.start()
+    scaling = scales[...]
+    for tile in range(mixed.shape[1] // LANES):
+        lanes = slice(tile * LANES, (tile + 1) * LANES)
+        normed[:, lanes] = (mixed[:, lanes] * scaling).astype(jnp.bfloat16)
+    normed_copy = pltpu.make_async_copy(normed, normed_out, sems.at[1])
+    normed_copy.start()
+    grads_copy.wait()
+    normed_copy.wait()
+
+
 def local(streams, short_taps, long_filter, skip_bias, norm_gain, cotangent):
     rows, chans = streams.shape[1], streams.shape[2]
     devices, groups = lax.axis_size("seq"), lax.axis_size("ch")
@@ -392,20 +457,20 @@
     vmem = [pltpu.VMEM(operand.shape, operand.dtype) for operand in operands]
     tail = 2 * ROWS
     exchanged = (5, devices * 2 * ROWS, rows)
-    return pl.pallas_call(
+    mixed, scales, grads = pl.pallas_call(
         functools.partial(operator_kernel, devices, groups),
         out_shape=(
-            jax.ShapeDtypeStruct((rows, chans), jnp.bfloat16),
+            jax.ShapeDtypeStruct((rows, chans), jnp.float32),
+            jax.ShapeDtypeStruct((rows, LANES), jnp.float32),
             jax.ShapeDtypeStruct(streams.shape, jnp.bfloat16),
         ),
         in_specs=[ANYWHERE] * len(operands),
-        out_specs=(WHOLE, WHOLE),
+        out_specs=(WHOLE, WHOLE, WHOLE),
         scratch_shapes=vmem
         + [
             pltpu.VMEM(exchanged, jnp.float32),
             pltpu.VMEM(exchanged, jnp.float32),
             pltpu.VMEM(streams.shape, jnp.float32),
-            pltpu.VMEM((rows, chans), jnp.float32),
             pltpu.VMEM((3, tail, chans), jnp.float32),
             pltpu.VMEM((2, ROWS, chans), jnp.float32),
             pltpu.VMEM((2, ROWS, chans), jnp.float32),
@@ -415,6 +480,7 @@
             pltpu.SemaphoreType.DMA((5,)),
             pltpu.SemaphoreType.DMA((5,)),
             pltpu.SemaphoreType.DMA((5,)),
+            pltpu.SemaphoreType.REGULAR,
             pltpu.SemaphoreType.DMA((1 + groups,)),
             pltpu.SemaphoreType.DMA((1 + groups,)),
         ],
@@ -422,6 +488,20 @@
             collective_id=0, has_side_effects=True, vmem_limit_bytes=48 << 20
         ),
     )(*(pltpu.with_memory_space_constraint(o, pltpu.HBM) for o in operands))
+    return pl.pallas_call(
+        closing_kernel,
+        out_shape=(
+            jax.ShapeDtypeStruct((rows, chans), jnp.bfloat16),
+            jax.ShapeDtypeStruct(streams.shape, jnp.bfloat16),
+        ),
+        in_specs=[WHOLE, WHOLE, WHOLE],
+        out_specs=(ANYWHERE, ANYWHERE),
+        scratch_shapes=[
+            pltpu.VMEM((rows, chans), jnp.bfloat16),
+            pltpu.SemaphoreType.DMA((2,)),
+        ],
+        compiler_params=pltpu.CompilerParams(vmem_limit_bytes=16 << 20),
+    )(mixed, scales, grads)
 
 
 def solution(mesh):

time: 78.1 us -> 75.6 us (0.968)
  the two profiles are of different devices: /device:TPU:1 before, /device:TPU:64 now
where the time goes in v4:
time: 75.6 us; the launch traced here: 75.5 us
  Pallas kernels  74.9 us (99%)
    pallas_call x1, Pallas kernels, local(): pl.pallas_call(functools.partial(operator_kernel, devices, groups), out_s...  73.9 us

profile of v4, /device:TPU:64, one launch (start us, length us, event | category | flops | bytes accessed | tf_op | source)
XLA Modules:
  0.0 75.5 jit_solution(6975065281183685988)
XLA Ops:
  0.6 73.9 %shard_map.122 = (f32[128,1024]{1,0:T(8,128)S(1)}, f32[128,128]{1,0:T(8,128)S(1)}, bf16[3,128,1024]{2,1,0:T(8,128)(2,1)S(1)}) custom-call(bf16[3,128,1024]{2,1,0:T(8,128)(2,1)} %streams_in.1, f32[3,3,1024]{2,1,0:T(4,128)} %taps_in.1, f32[128,1024]{1,0:T(8,128)} %filter_in.1, f32[1,1024]{1,0:T(1,128)} %bitcast.2, f32[1,1024]{1,0:T(1,128)} %bitcast.3, ...), custom_call_target="tpu_custom_call" | custom-call | tf_op jit(solution)/shard_map/pallas_call | solution.py:460
  74.5 1.0 %shard_map.123 = (bf16[128,1024]{1,0:T(8,128)(2,1)}, bf16[3,128,1024]{2,1,0:T(8,128)(2,1)}) custom-call(f32[128,1024]{1,0:T(8,128)S(1)} %get-tuple-element.5.mixed, f32[128,128]{1,0:T(8,128)S(1)} %get-tuple-element.6.scales, bf16[3,128,1024]{2,1,0:T(8,128)(2,1)S(1)} %get-tuple-element.7.grads), custom_call_target="tpu_custom_call" | custom-call | tf_op jit(solution)/shard_map/pallas_call | solution.py:491

commit v5 on v4

--- a/solution.py
+++ b/solution.py
@@ -162,6 +162,7 @@
     sent,
     got,
     shorts,
+    back_grad,
     edge,
     rim_sent,
     rim_got,
@@ -171,7 +172,7 @@
     send_sems,
     recv_sems,
     own_sems,
-    slab_sem,
+    slab_sems,
     small_send,
     small_recv,
 ):
@@ -186,16 +187,12 @@
     slabs = devices // SLAB
     slab, place = me // SLAB, me % SLAB
 
-    def within(i):
-        return slab * SLAB + (place + i) % SLAB
-
-    def across(i):
-        return (slab + i) % slabs * SLAB + place
-
-    for i in range(1, slabs):
-        pl.semaphore_signal(barrier, 1, device_id={"seq": across(i)}, device_id_type=MESH)
+    above, below = (me + SLAB) % devices, (me + devices - SLAB) % devices
     for i in range(1, SLAB):
-        pl.semaphore_signal(barrier, 1, device_id={"seq": within(i)}, device_id_type=MESH)
+        peer = slab * SLAB + (place + i) % SLAB
+        pl.semaphore_signal(barrier, 1, device_id={"seq": peer}, device_id_type=MESH)
+    for peer in (above, below):
+        pl.semaphore_signal(barrier, 1, device_id={"seq": peer}, device_id_type=MESH)
     for i in range(1, groups):
         pl.semaphore_signal(
             barrier, 1, device_id={"ch": (group + i) % groups}, device_id_type=MESH
@@ -271,6 +268,15 @@
             lax.fori_loop(0, SLAB, go, 0)
         return keep(phase)
 
+    def send_slab(phase, ahead, first_place):
+        base = (slab + ahead) % slabs * SLAB
+        send_all(phase, lambda i: base + (place + i) % SLAB, first_place, SLAB)
+
+    def report(way, step):
+        pl.semaphore_signal(
+            slab_sems.at[way, step], 1, device_id={"seq": (above, below)[way]}, device_id_type=MESH
+        )
+
     def exchange(phase):
         send_all(phase, lambda i: (me + i) % devices, 1, devices)
         return keep(phase)
@@ -291,9 +297,9 @@
     rim_sent[0] = jnp.zeros((ROWS, chans), jnp.float32)
     for i in range(3):
         rim_sent[0, 2 * i : 2 * i + 2, :] = streams[i, rows - 2 : rows, :].astype(jnp.float32)
-    pl.semaphore_wait(barrier, slabs + SLAB + groups - 3)
-    for i in range(1, slabs):
-        pl.semaphore_signal(slab_sem, 1, device_id={"seq": across(i)}, device_id_type=MESH)
+    pl.semaphore_wait(barrier, SLAB + groups)
+    report(0, 0)
+    report(1, 0)
 
     def rim_copy(which, peer):
         return pltpu.make_async_remote_copy(
@@ -305,17 +311,17 @@
             device_id_type=MESH,
         )
 
-    send_all(0, across, 1, slabs)
-    send_all(0, within, 1, SLAB)
-    pl.semaphore_wait(slab_sem, slabs - 1)
+    send_slab(0, 0, 1)
     halo_copy = rim_copy(0, (me + 1) % devices)
-    halo_copy.start()
-
-    def elsewhere(i):
-        ahead, beside = i % (slabs - 1) + 1, i // (slabs - 1) + 1
-        return (slab + ahead) % slabs * SLAB + (place + beside) % SLAB
-
-    send_all(0, elsewhere, 0, (slabs - 1) * (SLAB - 1))
+    last_step = slabs // 2 - 1
+    for step in range(last_step + 1):
+        for way in (1, 0) if step < last_step else (0,):
+            pl.semaphore_wait(slab_sems.at[way, step], 1)
+            if step + 1 < last_step or (step + 1 == last_step and way == 0):
+                report(way, step + 1)
+            if step == 0 and way == 1:
+                halo_copy.start()
+            send_slab(0, step + 1 if way else slabs - step - 1, 0)
     owns = [keep(0)]
     halo_copy.wait()
     for half in range(2):
@@ -357,37 +363,54 @@
     rim_sent[1] = jnp.zeros((ROWS, chans), jnp.float32)
     squares = jnp.zeros((rows, LANES), jnp.float32)
     tail = edge.shape[1]
-    for half in range(2):
-        arrive(3 + half, owns[3 + half])
-        for tile in range(half * tiles // 2, (half + 1) * tiles // 2):
-            lanes = lanes_of(tile)
-            start = tile % (tiles // 2) * per_tile
-            back = []
-            for s in range(2):
-                pieces = []
-                for i in range(per_tile):
-                    at = (start + i) * block + s * ROWS
-                    pieces.append(got[3 + half, at : at + ROWS, :])
-                back.append(jnp.transpose(jnp.concatenate(pieces, axis=0)))
-            short_q, short_k, short_v = (shorts[i, :, lanes] for i in range(3))
-            cot_wide = cot[:, lanes].astype(jnp.float32)
-            skip = bias[:, lanes]
-            direct = back[0] + skip * (short_k * short_v)
-            mix = short_q * direct
-            mixed[:, lanes] = mix * gain[:, lanes]
-            squares = squares + mix * mix
-            gated_grad = back[1] + skip * (cot_wide * short_q)
-            short_grad = (cot_wide * direct, gated_grad * short_v, gated_grad * short_k)
-            for i in range(3):
-                own = short_grad[i]
-                rim_sent[1, 2 * i : 2 * i + 2, lanes] = own[0:2]
-                once = jnp.where(places < rows - 1, pltpu.roll(own, rows - 1, axis=0), 0.0)
-                twice = jnp.where(places < rows - 2, pltpu.roll(own, rows - 2, axis=0), 0.0)
-                grad = (
-                    taps[i, 0:1, lanes] * own + taps[i, 1:2, lanes] * once + taps[i, 2:3, lanes] * twice
-                )
-                grads[i, : rows - tail, lanes] = grad[: rows - tail].astype(jnp.bfloat16)
-                edge[i, :, lanes] = grad[rows - tail :]
+
+    def cotangents(tile, direct, gated_grad):
+        lanes = lanes_of(tile)
+        return (
+            cot[: direct.shape[0], lanes].astype(jnp.float32) * direct,
+            gated_grad * shorts[2, : direct.shape[0], lanes],
+            gated_grad * shorts[1, : direct.shape[0], lanes],
+        )
+
+    def receive(half, tile):
+        lanes = lanes_of(tile)
+        start = tile % (tiles // 2) * per_tile
+        back = []
+        for s in range(2):
+            pieces = []
+            for i in range(per_tile):
+                at = (start + i) * block + s * ROWS
+                pieces.append(got[3 + half, at : at + ROWS, :])
+            back.append(jnp.transpose(jnp.concatenate(pieces, axis=0)))
+        short_q, short_k, short_v = (shorts[i, :, lanes] for i in range(3))
+        skip = bias[:, lanes]
+        direct = back[0] + skip * (short_k * short_v)
+        mix = short_q * direct
+        mixed[:, lanes] = mix * gain[:, lanes]
+        gated_grad = back[1] + skip * (cot[:, lanes].astype(jnp.float32) * short_q)
+        for i, rim in enumerate(cotangents(tile, direct[: 2 * ROWS], gated_grad[: 2 * ROWS])):
+            rim_sent[1, 2 * i : 2 * i + 2, lanes] = rim[0:2]
+        shorts[0, :, lanes] = direct
+        back_grad[:, lanes] = gated_grad
+        return mix * mix
+
+    def spread(tile):
+        lanes = lanes_of(tile)
+        for i, own in enumerate(cotangents(tile, shorts[0, :, lanes], back_grad[:, lanes])):
+            once = jnp.where(places < rows - 1, pltpu.roll(own, rows - 1, axis=0), 0.0)
+            twice = jnp.where(places < rows - 2, pltpu.roll(own, rows - 2, axis=0), 0.0)
+            grad = taps[i, 0:1, lanes] * own + taps[i, 1:2, lanes] * once + taps[i, 2:3, lanes] * twice
+            grads[i, : rows - tail, lanes] = grad[: rows - tail].astype(jnp.bfloat16)
+            edge[i, :, lanes] = grad[rows - tail :]
+
+    arrive(3, owns[3])
+    for tile in range(tiles // 2):
+        squares = squares + receive(0, tile)
+    for tile in range(tiles // 2):
+        spread(tile)
+    arrive(4, owns[4])
+    for tile in range(tiles // 2, tiles):
+        squares = squares + receive(1, tile)
 
     rim_back = rim_copy(1, (me + devices - 1) % devices)
     rim_back.start()
@@ -405,6 +428,8 @@
         )
         copy.start()
         copies.append(copy)
+    for tile in range(tiles // 2, tiles):
+        spread(tile)
     for copy in copies:
         copy.wait()
     for i in range(1, groups):
@@ -471,6 +496,7 @@
             pltpu.VMEM(exchanged, jnp.float32),
             pltpu.VMEM(exchanged, jnp.float32),
             pltpu.VMEM(streams.shape, jnp.float32),
+            pltpu.VMEM((rows, chans), jnp.float32),
             pltpu.VMEM((3, tail, chans), jnp.float32),
             pltpu.VMEM((2, ROWS, chans), jnp.float32),
             pltpu.VMEM((2, ROWS, chans), jnp.float32),
@@ -480,7 +506,7 @@
             pltpu.SemaphoreType.DMA((5,)),
             pltpu.SemaphoreType.DMA((5,)),
             pltpu.SemaphoreType.DMA((5,)),
-            pltpu.SemaphoreType.REGULAR,
+            pltpu.SemaphoreType.REGULAR((2, devices // SLAB // 2)),
             pltpu.SemaphoreType.DMA((1 + groups,)),
             pltpu.SemaphoreType.DMA((1 + groups,)),
         ],

time: 75.6 us -> 74.8 us (0.989)
  the two profiles are of different devices: /device:TPU:64 before, /device:TPU:1 now
where the time goes in v5:
time: 74.8 us; the launch traced here: 74.2 us
  Pallas kernels  73.6 us (98%)
    pallas_call x1, Pallas kernels, local(): pl.pallas_call(functools.partial(operator_kernel, devices, groups), out_s...  72.6 us

profile of v5, /device:TPU:1, one launch (start us, length us, event | category | flops | bytes accessed | tf_op | source)
XLA Modules:
  0.0 74.2 jit_solution(17507041541862920166)
XLA Ops:
  0.6 72.6 %shard_map.122 = (f32[128,1024]{1,0:T(8,128)S(1)}, f32[128,128]{1,0:T(8,128)S(1)}, bf16[3,128,1024]{2,1,0:T(8,128)(2,1)S(1)}) custom-call(bf16[3,128,1024]{2,1,0:T(8,128)(2,1)} %streams_in.1, f32[3,3,1024]{2,1,0:T(4,128)} %taps_in.1, f32[128,1024]{1,0:T(8,128)} %filter_in.1, f32[1,1024]{1,0:T(1,128)} %bitcast.2, f32[1,1024]{1,0:T(1,128)} %bitcast.3, ...), custom_call_target="tpu_custom_call" | custom-call | tf_op jit(solution)/shard_map/pallas_call | solution.py:485
  73.3 1.0 %shard_map.123 = (bf16[128,1024]{1,0:T(8,128)(2,1)}, bf16[3,128,1024]{2,1,0:T(8,128)(2,1)}) custom-call(f32[128,1024]{1,0:T(8,128)S(1)} %get-tuple-element.5.mixed, f32[128,128]{1,0:T(8,128)S(1)} %get-tuple-element.6.scales, bf16[3,128,1024]{2,1,0:T(8,128)(2,1)S(1)} %get-tuple-element.7.grads), custom_call_target="tpu_custom_call" | custom-call | tf_op jit(solution)/shard_map/pallas_call | solution.py:517

commit v6 on v5

--- a/solution.py
+++ b/solution.py
@@ -12,7 +12,7 @@
 LANES = 128
 ROWS = 8
 SLAB = 8
-SLAB_ORDER = (0, 1, 2, 3, 6, 7, 4, 5)
+SLAB_ORDER = ((0,), (1, 2), (3, 6, 7), (4, 5))
 MESH = pl.DeviceIdType.MESH
 WHOLE = pl.BlockSpec(memory_space=pltpu.VMEM)
 ANYWHERE = pl.BlockSpec(memory_space=pltpu.HBM)
@@ -254,14 +254,15 @@
         lax.fori_loop(start, stop, go, 0)
 
     def hand_back(phase):
-        for target in SLAB_ORDER:
+        for targets in SLAB_ORDER:
 
             def go(i, carry):
-                peer = target * SLAB + (place + i) % SLAB
-
-                @pl.when(peer != me)
-                def _():
-                    send(phase, peer)
+                for target in targets:
+                    peer = target * SLAB + (place + i) % SLAB
+
+                    @pl.when(peer != me)
+                    def _():
+                        send(phase, peer)
 
                 return carry
 
@@ -302,9 +303,14 @@
     report(1, 0)
 
     def rim_copy(which, peer):
+        if which == 0:
+            at = (0,)
+        else:
+            width = chans // 2
+            at = (1, slice(None), slice((which - 1) * width, which * width))
         return pltpu.make_async_remote_copy(
-            src_ref=rim_sent.at[which],
-            dst_ref=rim_got.at[which],
+            src_ref=rim_sent.at[at],
+            dst_ref=rim_got.at[at],
             send_sem=small_send.at[which],
             recv_sem=small_recv.at[which],
             device_id={"seq": peer},
@@ -403,42 +409,9 @@
             grads[i, : rows - tail, lanes] = grad[: rows - tail].astype(jnp.bfloat16)
             edge[i, :, lanes] = grad[rows - tail :]
 
-    arrive(3, owns[3])
-    for tile in range(tiles // 2):
-        squares = squares + receive(0, tile)
-    for tile in range(tiles // 2):
-        spread(tile)
-    arrive(4, owns[4])
-    for tile in range(tiles // 2, tiles):
-        squares = squares + receive(1, tile)
-
-    rim_back = rim_copy(1, (me + devices - 1) % devices)
-    rim_back.start()
-    total = jnp.sum(jnp.transpose(squares), axis=0, keepdims=True)
-    squares_sent[...] = jnp.broadcast_to(total, squares_sent.shape)
-    copies = []
-    for i in range(1, groups):
-        copy = pltpu.make_async_remote_copy(
-            src_ref=squares_sent,
-            dst_ref=squares_got.at[i - 1],
-            send_sem=small_send.at[1 + i],
-            recv_sem=small_recv.at[1 + i],
-            device_id={"ch": (group + i) % groups},
-            device_id_type=MESH,
-        )
-        copy.start()
-        copies.append(copy)
-    for tile in range(tiles // 2, tiles):
-        spread(tile)
-    for copy in copies:
-        copy.wait()
-    for i in range(1, groups):
-        total = total + squares_got[i - 1, 0:1, :]
-    scaling = lax.rsqrt(total / (chans * groups) + 1e-06)
-    scales[...] = jnp.transpose(jnp.broadcast_to(scaling, (LANES, rows)))
-    rim_back.wait()
     last_places = lax.broadcasted_iota(jnp.int32, (tail, LANES), 0)
-    for tile in range(tiles):
+
+    def finish(tile):
         lanes = lanes_of(tile)
         halo = jnp.where(me < devices - 1, rim_got[1, :, lanes], 0.0)
         for i in range(3):
@@ -450,6 +423,48 @@
                 jnp.where(last_places == tail - 2, third * near, 0.0),
             )
             grads[i, rows - tail :, lanes] = (edge[i, :, lanes] + more).astype(jnp.bfloat16)
+
+    arrive(3, owns[3])
+    for tile in range(tiles // 2):
+        squares = squares + receive(0, tile)
+    rims_back = [rim_copy(1, (me + devices - 1) % devices)]
+    rims_back[0].start()
+    for tile in range(tiles // 2):
+        spread(tile)
+    arrive(4, owns[4])
+    for tile in range(tiles // 2, tiles):
+        squares = squares + receive(1, tile)
+
+    total = jnp.sum(jnp.transpose(squares), axis=0, keepdims=True)
+    squares_sent[...] = jnp.broadcast_to(total, squares_sent.shape)
+    copies = []
+    for i in range(1, groups):
+        copy = pltpu.make_async_remote_copy(
+            src_ref=squares_sent,
+            dst_ref=squares_got.at[i - 1],
+            send_sem=small_send.at[2 + i],
+            recv_sem=small_recv.at[2 + i],
+            device_id={"ch": (group + i) % groups},
+            device_id_type=MESH,
+        )
+        copy.start()
+        copies.append(copy)
+    rims_back.append(rim_copy(2, (me + devices - 1) % devices))
+    rims_back[1].start()
+    for tile in range(tiles // 2, tiles):
+        spread(tile)
+    rims_back[0].wait()
+    for tile in range(tiles // 2):
+        finish(tile)
+    for copy in copies:
+        copy.wait()
+    for i in range(1, groups):
+        total = total + squares_got[i - 1, 0:1, :]
+    scaling = lax.rsqrt(total / (chans * groups) + 1e-06)
+    scales[...] = jnp.transpose(jnp.broadcast_to(scaling, (LANES, rows)))
+    rims_back[1].wait()
+    for tile in range(tiles // 2, tiles):
+        finish(tile)
     for phase in range(5):
         await_bytes(others(sent, phase), send_sems.at[phase])
 
@@ -507,8 +522,8 @@
             pltpu.SemaphoreType.DMA((5,)),
             pltpu.SemaphoreType.DMA((5,)),
             pltpu.SemaphoreType.REGULAR((2, devices // SLAB // 2)),
-            pltpu.SemaphoreType.DMA((1 + groups,)),
-            pltpu.SemaphoreType.DMA((1 + groups,)),
+            pltpu.SemaphoreType.DMA((2 + groups,)),
+            pltpu.SemaphoreType.DMA((2 + groups,)),
         ],
         compiler_params=pltpu.CompilerParams(
             collective_id=0, has_side_effects=True, vmem_limit_bytes=48 << 20

time: 74.8 us -> 74.3 us (level)
  no operation moved by 1% of the time
where the time goes in v6:
time: 74.3 us; the launch traced here: 74.1 us
  Pallas kernels  73.4 us (99%)
    pallas_call x1, Pallas kernels, local(): pl.pallas_call(functools.partial(operator_kernel, devices, groups), out_s...  72.4 us

profile of v6, /device:TPU:1, one launch (start us, length us, event | category | flops | bytes accessed | tf_op | source)
XLA Modules:
  0.0 74.1 jit_solution(1549662075794940272)
XLA Ops:
  0.6 72.4 %shard_map.122 = (f32[128,1024]{1,0:T(8,128)S(1)}, f32[128,128]{1,0:T(8,128)S(1)}, bf16[3,128,1024]{2,1,0:T(8,128)(2,1)S(1)}) custom-call(bf16[3,128,1024]{2,1,0:T(8,128)(2,1)} %streams_in.1, f32[3,3,1024]{2,1,0:T(4,128)} %taps_in.1, f32[128,1024]{1,0:T(8,128)} %filter_in.1, f32[1,1024]{1,0:T(1,128)} %bitcast.2, f32[1,1024]{1,0:T(1,128)} %bitcast.3, ...), custom_call_target="tpu_custom_call" | custom-call | tf_op jit(solution)/shard_map/pallas_call | solution.py:500
  73.1 1.0 %shard_map.123 = (bf16[128,1024]{1,0:T(8,128)(2,1)}, bf16[3,128,1024]{2,1,0:T(8,128)(2,1)}) custom-call(f32[128,1024]{1,0:T(8,128)S(1)} %get-tuple-element.5.mixed, f32[128,128]{1,0:T(8,128)S(1)} %get-tuple-element.6.scales, bf16[3,128,1024]{2,1,0:T(8,128)(2,1)S(1)} %get-tuple-element.7.grads), custom_call_target="tpu_custom_call" | custom-call | tf_op jit(solution)/shard_map/pallas_call | solution.py:532

commit v7 on v6

--- a/solution.py
+++ b/solution.py
@@ -279,7 +279,7 @@
         )
 
     def exchange(phase):
-        send_all(phase, lambda i: (me + i) % devices, 1, devices)
+        send_all(phase, lambda i: (me + i % slabs * SLAB + i // slabs) % devices, 1, devices)
         return keep(phase)
 
     def others(ref, phase):

time: 74.3 us -> 74.4 us (level); the launches traced: 74.1 us -> 73.3 us
    pallas_call x1, Pallas kernels: 72.4 us -> 71.7 us  [local(): pl.pallas_call(functools.partial(operator_kernel, devices, groups), out_s...]
where the time goes in v7:
time: 74.4 us; the launch traced here: 73.3 us
  Pallas kernels  72.7 us (98%)
    pallas_call x1, Pallas kernels, local(): pl.pallas_call(functools.partial(operator_kernel, devices, groups), out_s...  71.7 us

profile of v7, /device:TPU:1, one launch (start us, length us, event | category | flops | bytes accessed | tf_op | source)
XLA Modules:
  0.0 73.3 jit_solution(2526204027267147744)
XLA Ops:
  0.6 71.7 %shard_map.122 = (f32[128,1024]{1,0:T(8,128)S(1)}, f32[128,128]{1,0:T(8,128)S(1)}, bf16[3,128,1024]{2,1,0:T(8,128)(2,1)S(1)}) custom-call(bf16[3,128,1024]{2,1,0:T(8,128)(2,1)} %streams_in.1, f32[3,3,1024]{2,1,0:T(4,128)} %taps_in.1, f32[128,1024]{1,0:T(8,128)} %filter_in.1, f32[1,1024]{1,0:T(1,128)} %bitcast.2, f32[1,1024]{1,0:T(1,128)} %bitcast.3, ...), custom_call_target="tpu_custom_call" | custom-call | tf_op jit(solution)/shard_map/pallas_call | solution.py:500
  72.3 1.0 %shard_map.123 = (bf16[128,1024]{1,0:T(8,128)(2,1)}, bf16[3,128,1024]{2,1,0:T(8,128)(2,1)}) custom-call(f32[128,1024]{1,0:T(8,128)S(1)} %get-tuple-element.5.mixed, f32[128,128]{1,0:T(8,128)S(1)} %get-tuple-element.6.scales, bf16[3,128,1024]{2,1,0:T(8,128)(2,1)S(1)} %get-tuple-element.7.grads), custom_call_target="tpu_custom_call" | custom-call | tf_op jit(solution)/shard_map/pallas_call | solution.py:532
